TPU v7x, 32 devices: a whole 2x2x4 slice. The times are simulated.
32 devices in a mesh: row: 16 (over z, x, core), col: 2 (over y).
Axes of the slice: x: 2, y: 2, z: 4, core: 2. Of those that a mesh axis runs over, the one named last changes fastest.
Arguments:
- features: bfloat16 [8192, 256], P(('row', 'col')), may hold values from -6 to 6
- degrees: int32 [8192], P(('row', 'col')), may hold values from 1 to 64
- blocks: bfloat16 [256, 16, 128, 128], P('row', 'col'), may hold values from 0 to 2
- block_ids: int32 [256, 16], P('row', 'col'), may hold values from 0 to 7, as said below
- counts: int32 [256, 2], P('row', 'col'), may hold values from 1 to 8, as said below
- weight: bfloat16 [256, 256], replicated, may hold values from -0.375 to 0.375
- out_bias: float32 [256], replicated, may hold values from -3 to 3
Outputs:
- mixed: bfloat16 [8192, 256], P(('row', 'col'))
Inputs may be any that keep to these rules, and one draw needn't show every extreme that they name: `block_ids`: within each list of 8 slots (live or not) the codes are distinct. `counts`: every tile has one segment whose list is full.
All inputs are finite; a program needn't handle non-finite values.
Results may differ from a plain program's by a relative error of at most 0.018.
Values may be sent and summed in bfloat16 or wider, within the bound.
No kernel may reach another device: no remote copies, remote signals or barrier semaphores. Data moves between devices by JAX's collectives and lax.ppermute only.
A program may use at most 128 MiB of HBM per device.

v0:
```python
import functools

import jax
import jax.numpy as jnp
from jax import lax
from jax.experimental import pallas as pl
from jax.experimental.pallas import tpu as pltpu
from jax.sharding import PartitionSpec as P


def swap_with(value, axis, flip):
    size = lax.axis_size(axis)
    return lax.ppermute(value, axis, [(i, i ^ flip) for i in range(size)])


def from_ahead(value, axis, distance):
    size = lax.axis_size(axis)
    return lax.ppermute(value, axis, [((i + distance) % size, i) for i in range(size)])


def split_code(code, count):
    if count & (count - 1) == 0:
        return code >> (count.bit_length() - 1), code & (count - 1)
    return lax.div(code, count), lax.rem(code, count)


def arrange_kernel(orders, geometry, ids_hbm, counts_hbm, blocks_hbm, features_hbm, degrees_hbm, *rest):
    side, row_blocks, col_blocks, cols = geometry
    outs, rest = rest[: len(orders)], rest[len(orders) :]
    features_out, degrees_out, ids, counts, stage, sems, table_sems = rest
    slots = stage.shape[1]
    me = lax.axis_index("row")
    shift = (cols - lax.axis_index("col")) * (col_blocks // cols)

    flat = [me ^ delta for order in orders for delta in order]
    tables = [
        pltpu.make_async_copy(ids_hbm, ids, table_sems.at[0]),
        pltpu.make_async_copy(counts_hbm, counts, table_sems.at[1]),
    ]
    passed = [
        pltpu.make_async_copy(features_hbm, features_out, table_sems.at[2]),
        pltpu.make_async_copy(degrees_hbm, degrees_out, table_sems.at[3]),
    ]
    for table in tables:
        table.start()

    def fetch(spot):
        return pltpu.make_async_copy(blocks_hbm.at[flat[spot]], stage.at[spot], sems.at[spot])

    for spot in range(len(flat)):
        fetch(spot).start()
    for copy in passed:
        copy.start()
    if slots != row_blocks * col_blocks:
        for out in outs:
            out[...] = jnp.zeros(out.shape, out.dtype)
    for table in tables:
        table.wait()
    spot = 0
    for out, order in zip(outs, orders):
        for position in range(len(order)):
            segment = flat[spot]
            live = counts[0, segment]
            fetch(spot).wait()
            for slot in range(slots):
                down, across = split_code(ids[slot, segment], col_blocks)
                _, across = split_code(across + shift, col_blocks)
                values = stage[spot, slot]
                values = jnp.where(slot < live, values, jnp.zeros_like(values))
                rows = pl.ds(pl.multiple_of((position * row_blocks + down) * side, side), side)
                lanes = pl.ds(pl.multiple_of(across * side, side), side)
                out[rows, lanes] = values
            spot += 1
    for copy in passed:
        copy.wait()


def arrange(blocks, block_ids, counts, features, degrees, orders, group_rows):
    seg_rows = features.shape[0]
    segments, slots, side, _ = blocks.shape
    geometry = (side, seg_rows // side, group_rows // side, group_rows // seg_rows)
    total = sum(len(order) for order in orders)
    nbytes = total * seg_rows * group_rows * blocks.dtype.itemsize
    held = nbytes + total * slots * side * side * blocks.dtype.itemsize
    return pl.pallas_call(
        functools.partial(arrange_kernel, orders, geometry),
        out_shape=[jax.ShapeDtypeStruct((len(order) * seg_rows, group_rows), blocks.dtype) for order in orders]
        + [jax.ShapeDtypeStruct(v.shape, v.dtype) for v in (features, degrees)],
        in_specs=[pl.BlockSpec(memory_space=pltpu.HBM)] * 5,
        out_specs=[pl.BlockSpec(memory_space=pltpu.VMEM)] * (len(orders) + 2),
        scratch_shapes=[
            pltpu.SMEM((slots, segments), block_ids.dtype),
            pltpu.SMEM((1, segments), counts.dtype),
            pltpu.VMEM((total, slots, side, side), blocks.dtype),
            pltpu.SemaphoreType.DMA((total,)),
            pltpu.SemaphoreType.DMA((4,)),
        ],
        compiler_params=pltpu.CompilerParams(vmem_limit_bytes=held + (4 << 20)),
        cost_estimate=pl.CostEstimate(flops=0, bytes_accessed=2 * nbytes, transcendentals=0),
    )(*[
        pltpu.with_memory_space_constraint(v, pltpu.HBM)
        for v in (block_ids.T, counts.T, blocks, features, degrees)
    ])


def add(*values):
    return functools.reduce(jnp.add, [v.astype(jnp.float32) for v in values])


def narrow(value):
    return value.astype(jnp.bfloat16)


def local(features, degrees, blocks, block_ids, counts, weight, out_bias):
    seg_rows, width = features.shape
    rows, cols = lax.axis_size("row"), lax.axis_size("col")
    high = rows // 8

    moved = []
    for step in range(1, cols):
        features_in = from_ahead(features, "col", step)
        degrees_in = from_ahead(degrees, "col", step)
        moved.append((features_in, degrees_in))

    first = [h * 8 + q * 2 for q in (1, 2, 3) for h in range(1, high)]
    rest = [h * 8 for h in range(1, high)] + [q * 2 for q in range(4)]
    orders = [[delta | other for delta in part] for part in (first, rest) for other in (1, 0)]
    *dense, features, degrees = arrange(
        blocks, block_ids, counts, features, degrees, orders, cols * seg_rows
    )

    def scale(rows_in, counts_in):
        scaling = lax.rsqrt(counts_in.astype(jnp.float32))[:, None]
        return lax.optimization_barrier((rows_in.astype(jnp.float32) * scaling).astype(jnp.bfloat16))

    parts = [scale(features, degrees)] + [scale(*pair) for pair in moved]
    gathered = jnp.concatenate(parts, axis=0)

    def term(matrix):
        product = jnp.dot(matrix, gathered, preferred_element_type=jnp.float32).astype(jnp.bfloat16)
        return product.reshape(-1, seg_rows, width)

    def over_cores(mine, others):
        to_send = term(others)
        sent = swap_with(to_send, "row", 1)
        kept = term(mine)
        return narrow(add(kept, sent))

    chip_first = over_cores(dense[1], dense[0]).reshape(3, high - 1, seg_rows, width)
    got_far = []
    for q in (1, 3, 2):
        got_far.append(swap_with(chip_first[q - 1], "row", 2 * q))

    chip_rest = over_cores(dense[3], dense[2])
    chip_far, chip_near = chip_rest[: high - 1], chip_rest[high - 1 :]
    quad_far = narrow(add(chip_far, *got_far))
    across = []
    for h in range(1, high):
        across.append(swap_with(quad_far[h - 1], "row", 8 * h))

    got_near = []
    for q in (1, 3, 2):
        got_near.append(swap_with(chip_near[q], "row", 2 * q))

    own = add(chip_near[0], *got_near, *across)
    scaling = lax.rsqrt(degrees.astype(jnp.float32))[:, None]
    combined = (scaling * (own + parts[0].astype(jnp.float32))).astype(jnp.bfloat16)
    mixed = jnp.dot(combined, weight, preferred_element_type=jnp.float32) + out_bias
    return jnp.maximum(mixed, 0.0).astype(jnp.bfloat16)


def solution(mesh):
    placed = (
        P(("row", "col"), None),
        P(("row", "col")),
        P("row", "col", None, None),
        P("row", "col"),
        P("row", "col"),
        P(),
        P(),
    )

    return jax.shard_map(local, mesh=mesh, in_specs=placed, out_specs=P(("row", "col"), None), check_vma=False)
```

profile of v0, /device:TPU:0, one launch (start us, length us, event | category | flops | bytes accessed | tf_op | source)
XLA Modules:
  0.0 33.2 jit_solution(968274139517364185)
XLA Ops:
  0.0 0.0 copy-start
  0.0 3.0 %collective-permute-start = (bf16[256,256]{1,0:T(8,128)(2,1)}, bf16[256,256]{1,0:T(8,128)(2,1)S(1)}, u32[]{:S(2)}, u32[]{:S(2)}) collective-permute-start(bf16[256,256]{1,0:T(8,128)(2,1)} %features_hbm.1), channel_id=1, source_target_pairs={{1,0},{0,1},{3,2},{2,3},{5,4},{4,5},{7,6},{6,7},{9,8},{8,9},{11,10... | collective-permute-start | bytes 393224 | tf_op jit(solution)/shard_map/ppermute | solution.py:18
  3.0 0.1 collective-permute-start.1
  3.1 2.4 %shard_map.73 = (bf16[768,512]{1,0:T(8,128)(2,1)S(1)}, bf16[768,512]{1,0:T(8,128)(2,1)S(1)}, bf16[1280,512]{1,0:T(8,128)(2,1)S(1)}, bf16[1280,512]{1,0:T(8,128)(...) custom-call(s32[8,16]{1,0:T(8,128)} %bitcast.29, s32[1,16]{1,0:T(1,128)} %bitcast.30, ...), custom_call_target="tpu_custom_call" | custom-call | bytes 8388608 | tf_op jit(solution)/shard_map/pallas_call | solution.py:85
  5.5 0.1 multiply_convert_fusion.1
  5.6 1.2 %collective-permute-done.1 = s32[256]{0:T(256)S(1)} collective-permute-done((s32[256]{0:T(256)}, s32[256]{0:T(256)S(1)}, u32[]{:S(2)}, u32[]{:S(2)}) %collective-permute-start.1) | collective-permute-done | bytes 1056 | tf_op jit(solution)/shard_map/ppermute | solution.py:18
  6.8 0.0 collective-permute-done
  6.8 0.1 multiply_convert_fusion
  6.9 0.4 %convolution_convert_fusion.2 = bf16[768,256]{1,0:T(8,128)(2,1)S(1)} fusion(bf16[768,512]{1,0:T(8,128)(2,1)S(1)} %get-tuple-element.16, bf16[256,256]{1,0:T(8,128)(2,1)S(1)} %multiply_convert_fusion, bf16[256,256]{1,0:T(8,128)(2,1)S(1)} %multiply_convert_fusion.1), kind=kOutput, calls=%fused_computation.4 | convolution fusion | flops 202047488 | bytes 1441792 | tf_op jit(solution)/shard_map/dot_general | solution.py:140
  7.3 0.1 collective-permute-start.6
  7.3 0.5 %convolution_convert_fusion = bf16[1280,256]{1,0:T(8,128)(2,1)S(1)} fusion(bf16[1280,512]{1,0:T(8,128)(2,1)S(1)} %get-tuple-element.14, bf16[256,256]{1,0:T(8,128)(2,1)S(1)} %multiply_convert_fusion, bf16[256,256]{1,0:T(8,128)(2,1)S(1)} %multiply_convert_fusion.1), kind=kOutput, calls=%fused_computation | convolution fusion | flops 336396288 | bytes 2228224 | tf_op jit(solution)/shard_map/dot_general | solution.py:140
  7.9 0.6 %collective-permute-start.2 = (bf16[5,256,256]{2,1,0:T(8,128)(2,1)S(1)}, bf16[5,256,256]{2,1,0:T(8,128)(2,1)S(1)}, u32[]{:S(2)}, u32[]{:S(2)}) collective-permute-start(bf16[5,256,256]{2,1,0:T(8,128)(2,1)S(1)} %bitcast.31), channel_id=1, source_target_pairs={{0,2},{2,0},{4,6},{6,4},{8,10},{10,8},{12,14},{14,12},{16,18},{18,... | collective-permute-start | bytes 1966088 | tf_op jit(solution)/shard_map/ppermute | solution.py:13
  8.4 0.5 %convolution_convert_fusion.1 = bf16[1280,256]{1,0:T(8,128)(2,1)S(1)} fusion(bf16[1280,512]{1,0:T(8,128)(2,1)S(1)} %get-tuple-element.12, bf16[256,256]{1,0:T(8,128)(2,1)S(1)} %multiply_convert_fusion, bf16[256,256]{1,0:T(8,128)(2,1)S(1)} %multiply_convert_fusion.1), kind=kOutput, calls=%fused_computation.1 | convolution fusion | flops 336396288 | bytes 2228224 | tf_op jit(solution)/shard_map/dot_general | solution.py:140
  8.9 0.4 %convolution_convert_fusion.3 = bf16[768,256]{1,0:T(8,128)(2,1)S(1)} fusion(bf16[768,512]{1,0:T(8,128)(2,1)S(1)} %get-tuple-element.15, bf16[256,256]{1,0:T(8,128)(2,1)S(1)} %multiply_convert_fusion, bf16[256,256]{1,0:T(8,128)(2,1)S(1)} %multiply_convert_fusion.1), kind=kOutput, calls=%fused_computation.5 | convolution fusion | flops 202047488 | bytes 1441792 | tf_op jit(solution)/shard_map/dot_general | solution.py:140
  9.3 0.0 collective-permute-done.6
  9.3 0.1 fusion.3
  9.4 1.9 %collective-permute-start.9 = (bf16[1,256,256]{2,1,0:T(8,128)(2,1)S(1)}, bf16[1,256,256]{2,1,0:T(8,128)(2,1)S(1)}, u32[]{:S(2)}, u32[]{:S(2)}) collective-permute-start(bf16[1,256,256]{2,1,0:T(8,128)(2,1)S(1)} %get-tuple-element.21), channel_id=1, source_target_pairs={{0,8},{2,10},{4,12},{6,14},{8,0},{10,2},{12,4},{14,6},{16,24},{18,... | collective-permute-start | bytes 393224 | tf_op jit(solution)/shard_map/ppermute | solution.py:13
  11.3 1.4 %collective-permute-start.8 = (bf16[1,256,256]{2,1,0:T(8,128)(2,1)S(1)}, bf16[1,256,256]{2,1,0:T(8,128)(2,1)S(1)}, u32[]{:S(2)}, u32[]{:S(2)}) collective-permute-start(bf16[1,256,256]{2,1,0:T(8,128)(2,1)S(1)} %get-tuple-element.22), channel_id=1, source_target_pairs={{0,12},{2,14},{4,8},{6,10},{8,4},{10,6},{12,0},{14,2},{16,28},{18,... | collective-permute-start | bytes 393224 | tf_op jit(solution)/shard_map/ppermute | solution.py:13
  12.7 0.3 collective-permute-start.7
  13.0 0.0 collective-permute-done.2
  13.0 0.0 copy-start.1
  13.0 0.2 fusion
  13.2 2.2 %collective-permute-done.9 = bf16[1,256,256]{2,1,0:T(8,128)(2,1)S(1)} collective-permute-done((bf16[1,256,256]{2,1,0:T(8,128)(2,1)S(1)}, bf16[1,256,256]{2,1,0:T(8,128)(2,1)S(1)}, u32[]{:S(2)}, u32[]{:S(2)}) %collective-permute-start.9) | collective-permute-done | bytes 131104 | tf_op jit(solution)/shard_map/ppermute | solution.py:13
  15.4 3.6 %collective-permute-done.8 = bf16[1,256,256]{2,1,0:T(8,128)(2,1)S(1)} collective-permute-done((bf16[1,256,256]{2,1,0:T(8,128)(2,1)S(1)}, bf16[1,256,256]{2,1,0:T(8,128)(2,1)S(1)}, u32[]{:S(2)}, u32[]{:S(2)}) %collective-permute-start.8) | collective-permute-done | bytes 131104 | tf_op jit(solution)/shard_map/ppermute | solution.py:13
  19.0 1.4 %collective-permute-done.7 = bf16[1,256,256]{2,1,0:T(8,128)(2,1)S(1)} collective-permute-done((bf16[1,256,256]{2,1,0:T(8,128)(2,1)S(1)}, bf16[1,256,256]{2,1,0:T(8,128)(2,1)S(1)}, u32[]{:S(2)}, u32[]{:S(2)}) %collective-permute-start.7) | collective-permute-done | bytes 131104 | tf_op jit(solution)/shard_map/ppermute | solution.py:13
  20.3 0.1 fusion.10
  20.4 2.7 %collective-permute-start.10 = (bf16[256,256]{1,0:T(8,128)(2,1)S(1)}, bf16[256,256]{1,0:T(8,128)(2,1)S(1)}, u32[]{:S(2)}, u32[]{:S(2)}) collective-permute-start(bf16[256,256]{1,0:T(8,128)(2,1)S(1)} %fusion.10), channel_id=1, source_target_pairs={{0,16},{2,18},{4,20},{6,22},{8,24},{10,26},{12,28},{14,30},{16,0},... | collective-permute-start | bytes 393224 | tf_op jit(solution)/shard_map/ppermute | solution.py:13
  23.1 1.6 %collective-permute-start.5 = (bf16[256,256]{1,0:T(8,128)(2,1)S(1)}, bf16[256,256]{1,0:T(8,128)(2,1)S(1)}, u32[]{:S(2)}, u32[]{:S(2)}) collective-permute-start(bf16[256,256]{1,0:T(8,128)(2,1)S(1)} %get-tuple-element.18), channel_id=1, source_target_pairs={{0,8},{2,10},{4,12},{6,14},{8,0},{10,2},{12,4},{14,6},{16,24},{18,... | collective-permute-start | bytes 393224 | tf_op jit(solution)/shard_map/ppermute | solution.py:13
  24.6 0.4 %collective-permute-start.4 = (bf16[256,256]{1,0:T(8,128)(2,1)S(1)}, bf16[256,256]{1,0:T(8,128)(2,1)S(1)}, u32[]{:S(2)}, u32[]{:S(2)}) collective-permute-start(bf16[256,256]{1,0:T(8,128)(2,1)S(1)} %get-tuple-element.19), channel_id=1, source_target_pairs={{0,12},{2,14},{4,8},{6,10},{8,4},{10,6},{12,0},{14,2},{16,28},{18,... | collective-permute-start | bytes 393224 | tf_op jit(solution)/shard_map/ppermute | solution.py:13
  25.1 1.5 %collective-permute-start.3 = (bf16[256,256]{1,0:T(8,128)(2,1)S(1)}, bf16[256,256]{1,0:T(8,128)(2,1)S(1)}, u32[]{:S(2)}, u32[]{:S(2)}) collective-permute-start(bf16[256,256]{1,0:T(8,128)(2,1)S(1)} %get-tuple-element.17), channel_id=1, source_target_pairs={{0,4},{2,6},{4,0},{6,2},{8,12},{10,14},{12,8},{14,10},{16,20},{18,... | collective-permute-start | bytes 393224 | tf_op jit(solution)/shard_map/ppermute | solution.py:13
  26.6 2.2 %collective-permute-done.10 = bf16[256,256]{1,0:T(8,128)(2,1)S(1)} collective-permute-done((bf16[256,256]{1,0:T(8,128)(2,1)S(1)}, bf16[256,256]{1,0:T(8,128)(2,1)S(1)}, u32[]{:S(2)}, u32[]{:S(2)}) %collective-permute-start.10) | collective-permute-done | bytes 131104 | tf_op jit(solution)/shard_map/ppermute | solution.py:13
  28.7 1.7 %collective-permute-done.5 = bf16[256,256]{1,0:T(8,128)(2,1)S(1)} collective-permute-done((bf16[256,256]{1,0:T(8,128)(2,1)S(1)}, bf16[256,256]{1,0:T(8,128)(2,1)S(1)}, u32[]{:S(2)}, u32[]{:S(2)}) %collective-permute-start.5) | collective-permute-done | bytes 131104 | tf_op jit(solution)/shard_map/ppermute | solution.py:13
  30.5 1.3 %collective-permute-done.4 = bf16[256,256]{1,0:T(8,128)(2,1)S(1)} collective-permute-done((bf16[256,256]{1,0:T(8,128)(2,1)S(1)}, bf16[256,256]{1,0:T(8,128)(2,1)S(1)}, u32[]{:S(2)}, u32[]{:S(2)}) %collective-permute-start.4) | collective-permute-done | bytes 131104 | tf_op jit(solution)/shard_map/ppermute | solution.py:13
  31.7 0.5 %collective-permute-done.3 = bf16[256,256]{1,0:T(8,128)(2,1)S(1)} collective-permute-done((bf16[256,256]{1,0:T(8,128)(2,1)S(1)}, bf16[256,256]{1,0:T(8,128)(2,1)S(1)}, u32[]{:S(2)}, u32[]{:S(2)}) %collective-permute-start.3) | collective-permute-done | bytes 131104 | tf_op jit(solution)/shard_map/ppermute | solution.py:13
  32.3 0.0 copy-done
  32.3 0.0 copy-done.1
  32.3 0.9 %fusion.2 = bf16[256,256]{1,0:T(8,128)(2,1)} fusion(bf16[256,256]{1,0:T(8,128)(2,1)S(1)} %copy-done, bf16[256,256]{1,0:T(8,128)(2,1)S(1)} %multiply_convert_fusion.1, bf16[256,256]{1,0:T(8,128)(2,1)S(1)} %collective-permute-done.10, bf16[256,256]{1,0:T(8,128)(2,1)S(1)} %collective-permute-done.5, bf16[256,256]{1,0:T(8,128)(2,1)S(1)} %collective-permute-done.4, ...), kind=kOutput, calls=%fused_computation.8 | convolution fusion | flops 34603008 | bytes 1050624 | tf_op jit(solution)/shard_map/dot_general | solution.py:168
  (4 shorter events, 0.1 us)
Async XLA Ops:
  0.0 32.3 %copy-start = (bf16[256,256]{1,0:T(8,128)(2,1)S(1)}, bf16[256,256]{1,0:T(8,128)(2,1)}, u32[]{:S(2)}) copy-start(bf16[256,256]{1,0:T(8,128)(2,1)} %param.12) | copy-start | bytes 393220
  0.0 6.8 %collective-permute-start = (bf16[256,256]{1,0:T(8,128)(2,1)}, bf16[256,256]{1,0:T(8,128)(2,1)S(1)}, u32[]{:S(2)}, u32[]{:S(2)}) collective-permute-start(bf16[256,256]{1,0:T(8,128)(2,1)} %features_hbm.1), channel_id=1, source_target_pairs={{1,0},{0,1},{3,2},{2,3},{5,4},{4,5},{7,6},{6,7},{9,8},{8,9},{11,10... | collective-permute-start | bytes 393224 | tf_op jit(solution)/shard_map/ppermute | solution.py:18
  3.0 3.8 %collective-permute-start.1 = (s32[256]{0:T(256)}, s32[256]{0:T(256)S(1)}, u32[]{:S(2)}, u32[]{:S(2)}) collective-permute-start(s32[256]{0:T(256)} %degrees_hbm.1), channel_id=1, source_target_pairs={{1,0},{0,1},{3,2},{2,3},{5,4},{4,5},{7,6},{6,7},{9,8},{8,9},{11,10... | collective-permute-start | bytes 3080 | tf_op jit(solution)/shard_map/ppermute | solution.py:18
  7.3 2.0 %collective-permute-start.6 = (bf16[3,256,256]{2,1,0:T(8,128)(2,1)S(1)}, bf16[3,256,256]{2,1,0:T(8,128)(2,1)S(1)}, u32[]{:S(2)}, u32[]{:S(2)}) collective-permute-start(bf16[3,256,256]{2,1,0:T(8,128)(2,1)S(1)} %bitcast.32), channel_id=1, source_target_pairs={{0,2},{2,0},{4,6},{6,4},{8,10},{10,8},{12,14},{14,12},{16,18},{18,... | collective-permute-start | bytes 1179656 | tf_op jit(solution)/shard_map/ppermute | solution.py:13
  7.9 5.1 %collective-permute-start.2 = (bf16[5,256,256]{2,1,0:T(8,128)(2,1)S(1)}, bf16[5,256,256]{2,1,0:T(8,128)(2,1)S(1)}, u32[]{:S(2)}, u32[]{:S(2)}) collective-permute-start(bf16[5,256,256]{2,1,0:T(8,128)(2,1)S(1)} %bitcast.31), channel_id=1, source_target_pairs={{0,2},{2,0},{4,6},{6,4},{8,10},{10,8},{12,14},{14,12},{16,18},{18,... | collective-permute-start | bytes 1966088 | tf_op jit(solution)/shard_map/ppermute | solution.py:13
  9.4 5.9 %collective-permute-start.9 = (bf16[1,256,256]{2,1,0:T(8,128)(2,1)S(1)}, bf16[1,256,256]{2,1,0:T(8,128)(2,1)S(1)}, u32[]{:S(2)}, u32[]{:S(2)}) collective-permute-start(bf16[1,256,256]{2,1,0:T(8,128)(2,1)S(1)} %get-tuple-element.21), channel_id=1, source_target_pairs={{0,8},{2,10},{4,12},{6,14},{8,0},{10,2},{12,4},{14,6},{16,24},{18,... | collective-permute-start | bytes 393224 | tf_op jit(solution)/shard_map/ppermute | solution.py:13
  11.3 7.7 %collective-permute-start.8 = (bf16[1,256,256]{2,1,0:T(8,128)(2,1)S(1)}, bf16[1,256,256]{2,1,0:T(8,128)(2,1)S(1)}, u32[]{:S(2)}, u32[]{:S(2)}) collective-permute-start(bf16[1,256,256]{2,1,0:T(8,128)(2,1)S(1)} %get-tuple-element.22), channel_id=1, source_target_pairs={{0,12},{2,14},{4,8},{6,10},{8,4},{10,6},{12,0},{14,2},{16,28},{18,... | collective-permute-start | bytes 393224 | tf_op jit(solution)/shard_map/ppermute | solution.py:13
  12.7 7.7 %collective-permute-start.7 = (bf16[1,256,256]{2,1,0:T(8,128)(2,1)S(1)}, bf16[1,256,256]{2,1,0:T(8,128)(2,1)S(1)}, u32[]{:S(2)}, u32[]{:S(2)}) collective-permute-start(bf16[1,256,256]{2,1,0:T(8,128)(2,1)S(1)} %get-tuple-element.20), channel_id=1, source_target_pairs={{0,4},{2,6},{4,0},{6,2},{8,12},{10,14},{12,8},{14,10},{16,20},{18,... | collective-permute-start | bytes 393224 | tf_op jit(solution)/shard_map/ppermute | solution.py:13
  13.0 19.3 %copy-start.1 = (f32[256]{0:T(256)S(1)}, f32[256]{0:T(256)}, u32[]{:S(2)}) copy-start(f32[256]{0:T(256)} %param.13) | copy-start | bytes 3076
  20.4 8.3 %collective-permute-start.10 = (bf16[256,256]{1,0:T(8,128)(2,1)S(1)}, bf16[256,256]{1,0:T(8,128)(2,1)S(1)}, u32[]{:S(2)}, u32[]{:S(2)}) collective-permute-start(bf16[256,256]{1,0:T(8,128)(2,1)S(1)} %fusion.10), channel_id=1, source_target_pairs={{0,16},{2,18},{4,20},{6,22},{8,24},{10,26},{12,28},{14,30},{16,0},... | collective-permute-start | bytes 393224 | tf_op jit(solution)/shard_map/ppermute | solution.py:13
  23.1 7.4 %collective-permute-start.5 = (bf16[256,256]{1,0:T(8,128)(2,1)S(1)}, bf16[256,256]{1,0:T(8,128)(2,1)S(1)}, u32[]{:S(2)}, u32[]{:S(2)}) collective-permute-start(bf16[256,256]{1,0:T(8,128)(2,1)S(1)} %get-tuple-element.18), channel_id=1, source_target_pairs={{0,8},{2,10},{4,12},{6,14},{8,0},{10,2},{12,4},{14,6},{16,24},{18,... | collective-permute-start | bytes 393224 | tf_op jit(solution)/shard_map/ppermute | solution.py:13
  24.6 7.1 %collective-permute-start.4 = (bf16[256,256]{1,0:T(8,128)(2,1)S(1)}, bf16[256,256]{1,0:T(8,128)(2,1)S(1)}, u32[]{:S(2)}, u32[]{:S(2)}) collective-permute-start(bf16[256,256]{1,0:T(8,128)(2,1)S(1)} %get-tuple-element.19), channel_id=1, source_target_pairs={{0,12},{2,14},{4,8},{6,10},{8,4},{10,6},{12,0},{14,2},{16,28},{18,... | collective-permute-start | bytes 393224 | tf_op jit(solution)/shard_map/ppermute | solution.py:13
  25.1 7.2 %collective-permute-start.3 = (bf16[256,256]{1,0:T(8,128)(2,1)S(1)}, bf16[256,256]{1,0:T(8,128)(2,1)S(1)}, u32[]{:S(2)}, u32[]{:S(2)}) collective-permute-start(bf16[256,256]{1,0:T(8,128)(2,1)S(1)} %get-tuple-element.17), channel_id=1, source_target_pairs={{0,4},{2,6},{4,0},{6,2},{8,12},{10,14},{12,8},{14,10},{16,20},{18,... | collective-permute-start | bytes 393224 | tf_op jit(solution)/shard_map/ppermute | solution.py:13
where the time goes:
time: 33.3 us; the launch traced here: 33.2 us
  waiting for transfers between devices  14 us (42%)
  starting transfers between devices  13.4 us (40%)
  matrix products  2.64 us (8%)
  Pallas kernels  2.42 us (7%)
  other arithmetic  0.54 us (2%)
    ppermute x9, waiting for transfers between devices, swap_with(): return lax.ppermute(value, axis, [(i, i ^ flip) for i in range(size)])  12.9 us
    ppermute x9, starting transfers between devices, swap_with(): return lax.ppermute(value, axis, [(i, i ^ flip) for i in range(size)])  10.3 us
    ppermute x2, starting transfers between devices, from_ahead(): lax.ppermute(value, axis, [((i + distance) % size, i) for i in range(size)])  3.07 us
    pallas_call x1, Pallas kernels, arrange(): pl.pallas_call(functools.partial(arrange_kernel, orders, geometry), out_s...  2.42 us
    dot_general x4, matrix products, term(): jnp.dot(matrix, gathered, preferred_element_type=jnp.float32)  1.72 us
    ppermute x2, waiting for transfers between devices, from_ahead(): lax.ppermute(value, axis, [((i + distance) % size, i) for i in range(size)])  1.17 us
    dot_general x1, matrix products, local(): jnp.dot(combined, weight, preferred_element_type=jnp.float32) + out_bias  0.91 us
  transfers between devices with their start and end apart: 11, of which 8 were waited for; matrix products, arithmetic and copies ran while one was open for 5% of the time, Pallas kernels for 7%

commit v1 on v0

--- a/solution.py
+++ b/solution.py
@@ -134,11 +134,18 @@
         return lax.optimization_barrier((rows_in.astype(jnp.float32) * scaling).astype(jnp.bfloat16))
 
     parts = [scale(features, degrees)] + [scale(*pair) for pair in moved]
-    gathered = jnp.concatenate(parts, axis=0)
+    gathered = jnp.concatenate(parts[1:], axis=0)
 
-    def term(matrix):
-        product = jnp.dot(matrix, gathered, preferred_element_type=jnp.float32).astype(jnp.bfloat16)
-        return product.reshape(-1, seg_rows, width)
+    def product(matrix, features_in):
+        return jnp.dot(matrix, features_in, preferred_element_type=jnp.float32)
+
+    def term(at):
+        if at < 2:
+            ahead = lax.optimization_barrier(product(dense[at][:, :seg_rows], parts[0]))
+            total = ahead + product(dense[at][:, seg_rows:], gathered)
+        else:
+            total = product(dense[at], jnp.concatenate(parts, axis=0))
+        return narrow(total).reshape(-1, seg_rows, width)
 
     def over_cores(mine, others):
         to_send = term(others)
@@ -146,12 +153,12 @@
         kept = term(mine)
         return narrow(add(kept, sent))
 
-    chip_first = over_cores(dense[1], dense[0]).reshape(3, high - 1, seg_rows, width)
+    chip_first = over_cores(1, 0).reshape(3, high - 1, seg_rows, width)
     got_far = []
     for q in (1, 3, 2):
         got_far.append(swap_with(chip_first[q - 1], "row", 2 * q))
 
-    chip_rest = over_cores(dense[3], dense[2])
+    chip_rest = over_cores(3, 2)
     chip_far, chip_near = chip_rest[: high - 1], chip_rest[high - 1 :]
     quad_far = narrow(add(chip_far, *got_far))
     across = []

time: 33.3 us -> 30.1 us (0.904)
  the two profiles are of different devices: /device:TPU:0 before, /device:TPU:2 now
where the time goes in v1:
time: 30.1 us; the launch traced here: 30 us
  starting transfers between devices  12.4 us (41%)
  waiting for transfers between devices  11.4 us (38%)
  matrix products  2.98 us (10%)
  Pallas kernels  2.42 us (8%)
  other arithmetic  0.55 us (2%)
    ppermute x9, starting transfers between devices, swap_with(): return lax.ppermute(value, axis, [(i, i ^ flip) for i in range(size)])  10.4 us
    ppermute x9, waiting for transfers between devices, swap_with(): return lax.ppermute(value, axis, [(i, i ^ flip) for i in range(size)])  9.85 us
    pallas_call x1, Pallas kernels, arrange(): pl.pallas_call(functools.partial(arrange_kernel, orders, geometry), out_s...  2.42 us
    dot_general x6, matrix products, product(): return jnp.dot(matrix, features_in, preferred_element_type=jnp.float32)  2.06 us
    ppermute x2, starting transfers between devices, from_ahead(): lax.ppermute(value, axis, [((i + distance) % size, i) for i in range(size)])  2.03 us
    ppermute x2, waiting for transfers between devices, from_ahead(): lax.ppermute(value, axis, [((i + distance) % size, i) for i in range(size)])  1.57 us
    dot_general x1, matrix products, local(): jnp.dot(combined, weight, preferred_element_type=jnp.float32) + out_bias  0.92 us
  transfers between devices with their start and end apart: 11, of which 6 were waited for; matrix products, arithmetic and copies ran while one was open for 6% of the time, Pallas kernels for 8%

profile of v1, /device:TPU:2, one launch (start us, length us, event | category | flops | bytes accessed | tf_op | source)
XLA Modules:
  0.0 30.0 jit_solution(5528501180318802655)
XLA Ops:
  0.0 0.0 copy-start
  0.0 1.5 %collective-permute-start.1 = (s32[256]{0:T(256)}, s32[256]{0:T(256)S(1)}, u32[]{:S(2)}, u32[]{:S(2)}) collective-permute-start(s32[256]{0:T(256)} %degrees_hbm.1), channel_id=1, source_target_pairs={{1,0},{0,1},{3,2},{2,3},{5,4},{4,5},{7,6},{6,7},{9,8},{8,9},{11,10... | collective-permute-start | bytes 3080 | tf_op jit(solution)/shard_map/ppermute | solution.py:18
  1.5 0.5 %collective-permute-start = (bf16[256,256]{1,0:T(8,128)(2,1)}, bf16[256,256]{1,0:T(8,128)(2,1)S(1)}, u32[]{:S(2)}, u32[]{:S(2)}) collective-permute-start(bf16[256,256]{1,0:T(8,128)(2,1)} %features_hbm.1), channel_id=1, source_target_pairs={{1,0},{0,1},{3,2},{2,3},{5,4},{4,5},{7,6},{6,7},{9,8},{8,9},{11,10... | collective-permute-start | bytes 393224 | tf_op jit(solution)/shard_map/ppermute | solution.py:18
  2.0 2.4 %shard_map.73 = (bf16[768,512]{1,0:T(8,128)(2,1)S(1)}, bf16[768,512]{1,0:T(8,128)(2,1)S(1)}, bf16[1280,512]{1,0:T(8,128)(2,1)S(1)}, bf16[1280,512]{1,0:T(8,128)(...) custom-call(s32[8,16]{1,0:T(8,128)} %bitcast.32, s32[1,16]{1,0:T(1,128)} %bitcast.33, ...), custom_call_target="tpu_custom_call" | custom-call | bytes 8388608 | tf_op jit(solution)/shard_map/pallas_call | solution.py:85
  4.5 0.1 multiply_convert_fusion.1
  4.6 0.3 fusion.7
  4.8 0.3 fusion.10
  5.1 0.0 collective-permute-done.1
  5.1 1.6 %collective-permute-done = bf16[256,256]{1,0:T(8,128)(2,1)S(1)} collective-permute-done((bf16[256,256]{1,0:T(8,128)(2,1)}, bf16[256,256]{1,0:T(8,128)(2,1)S(1)}, u32[]{:S(2)}, u32[]{:S(2)}) %collective-permute-start) | collective-permute-done | bytes 131104 | tf_op jit(solution)/shard_map/ppermute | solution.py:18
  6.7 0.1 multiply_convert_fusion
  6.8 0.5 %convolution_convert_fusion = bf16[1280,256]{1,0:T(8,128)(2,1)S(1)} fusion(bf16[1280,512]{1,0:T(8,128)(2,1)S(1)} %get-tuple-element.14, bf16[256,256]{1,0:T(8,128)(2,1)S(1)} %multiply_convert_fusion, bf16[256,256]{1,0:T(8,128)(2,1)S(1)} %multiply_convert_fusion.1), kind=kOutput, calls=%fused_computation | convolution fusion | flops 336396288 | bytes 2228224 | tf_op jit(solution)/shard_map/dot_general | solution.py:140
  7.3 0.3 fusion.2
  7.6 0.1 collective-permute-start.6
  7.7 0.5 %convolution_convert_fusion.1 = bf16[1280,256]{1,0:T(8,128)(2,1)S(1)} fusion(bf16[1280,512]{1,0:T(8,128)(2,1)S(1)} %get-tuple-element.12, bf16[256,256]{1,0:T(8,128)(2,1)S(1)} %multiply_convert_fusion, bf16[256,256]{1,0:T(8,128)(2,1)S(1)} %multiply_convert_fusion.1), kind=kOutput, calls=%fused_computation.1 | convolution fusion | flops 336396288 | bytes 2228224 | tf_op jit(solution)/shard_map/dot_general | solution.py:140
  8.2 0.6 %collective-permute-start.2 = (bf16[5,256,256]{2,1,0:T(8,128)(2,1)S(1)}, bf16[5,256,256]{2,1,0:T(8,128)(2,1)S(1)}, u32[]{:S(2)}, u32[]{:S(2)}) collective-permute-start(bf16[5,256,256]{2,1,0:T(8,128)(2,1)S(1)} %bitcast.34), channel_id=1, source_target_pairs={{0,2},{2,0},{4,6},{6,4},{8,10},{10,8},{12,14},{14,12},{16,18},{18,... | collective-permute-start | bytes 1966088 | tf_op jit(solution)/shard_map/ppermute | solution.py:13
  8.7 0.3 fusion.1
  9.0 0.4 %collective-permute-done.6 = bf16[3,256,256]{2,1,0:T(8,128)(2,1)S(1)} collective-permute-done((bf16[3,256,256]{2,1,0:T(8,128)(2,1)S(1)}, bf16[3,256,256]{2,1,0:T(8,128)(2,1)S(1)}, u32[]{:S(2)}, u32[]{:S(2)}) %collective-permute-start.6) | collective-permute-done | bytes 393248 | tf_op jit(solution)/shard_map/ppermute | solution.py:13
  9.4 0.1 fusion.5
  9.5 0.6 %collective-permute-start.7 = (bf16[1,256,256]{2,1,0:T(8,128)(2,1)S(1)}, bf16[1,256,256]{2,1,0:T(8,128)(2,1)S(1)}, u32[]{:S(2)}, u32[]{:S(2)}) collective-permute-start(bf16[1,256,256]{2,1,0:T(8,128)(2,1)S(1)} %get-tuple-element.20), channel_id=1, source_target_pairs={{0,4},{2,6},{4,0},{6,2},{8,12},{10,14},{12,8},{14,10},{16,20},{18,... | collective-permute-start | bytes 393224 | tf_op jit(solution)/shard_map/ppermute | solution.py:13
  10.1 1.6 %collective-permute-start.9 = (bf16[1,256,256]{2,1,0:T(8,128)(2,1)S(1)}, bf16[1,256,256]{2,1,0:T(8,128)(2,1)S(1)}, u32[]{:S(2)}, u32[]{:S(2)}) collective-permute-start(bf16[1,256,256]{2,1,0:T(8,128)(2,1)S(1)} %get-tuple-element.21), channel_id=1, source_target_pairs={{0,8},{2,10},{4,12},{6,14},{8,0},{10,2},{12,4},{14,6},{16,24},{18,... | collective-permute-start | bytes 393224 | tf_op jit(solution)/shard_map/ppermute | solution.py:13
  11.7 1.4 %collective-permute-start.8 = (bf16[1,256,256]{2,1,0:T(8,128)(2,1)S(1)}, bf16[1,256,256]{2,1,0:T(8,128)(2,1)S(1)}, u32[]{:S(2)}, u32[]{:S(2)}) collective-permute-start(bf16[1,256,256]{2,1,0:T(8,128)(2,1)S(1)} %get-tuple-element.22), channel_id=1, source_target_pairs={{0,12},{2,14},{4,8},{6,10},{8,4},{10,6},{12,0},{14,2},{16,28},{18,... | collective-permute-start | bytes 393224 | tf_op jit(solution)/shard_map/ppermute | solution.py:13
  13.1 0.0 collective-permute-done.2
  13.1 0.0 copy-start.1
  13.1 0.2 fusion
  13.3 0.6 %collective-permute-start.3 = (bf16[256,256]{1,0:T(8,128)(2,1)S(1)}, bf16[256,256]{1,0:T(8,128)(2,1)S(1)}, u32[]{:S(2)}, u32[]{:S(2)}) collective-permute-start(bf16[256,256]{1,0:T(8,128)(2,1)S(1)} %get-tuple-element.17), channel_id=1, source_target_pairs={{0,4},{2,6},{4,0},{6,2},{8,12},{10,14},{12,8},{14,10},{16,20},{18,... | collective-permute-start | bytes 393224 | tf_op jit(solution)/shard_map/ppermute | solution.py:13
  13.9 1.6 %collective-permute-start.5 = (bf16[256,256]{1,0:T(8,128)(2,1)S(1)}, bf16[256,256]{1,0:T(8,128)(2,1)S(1)}, u32[]{:S(2)}, u32[]{:S(2)}) collective-permute-start(bf16[256,256]{1,0:T(8,128)(2,1)S(1)} %get-tuple-element.18), channel_id=1, source_target_pairs={{0,8},{2,10},{4,12},{6,14},{8,0},{10,2},{12,4},{14,6},{16,24},{18,... | collective-permute-start | bytes 393224 | tf_op jit(solution)/shard_map/ppermute | solution.py:13
  15.5 0.0 collective-permute-done.7
  15.5 1.4 %collective-permute-start.4 = (bf16[256,256]{1,0:T(8,128)(2,1)S(1)}, bf16[256,256]{1,0:T(8,128)(2,1)S(1)}, u32[]{:S(2)}, u32[]{:S(2)}) collective-permute-start(bf16[256,256]{1,0:T(8,128)(2,1)S(1)} %get-tuple-element.19), channel_id=1, source_target_pairs={{0,12},{2,14},{4,8},{6,10},{8,4},{10,6},{12,0},{14,2},{16,28},{18,... | collective-permute-start | bytes 393224 | tf_op jit(solution)/shard_map/ppermute | solution.py:13
  16.8 0.0 collective-permute-done.9
  16.8 3.4 %collective-permute-done.8 = bf16[1,256,256]{2,1,0:T(8,128)(2,1)S(1)} collective-permute-done((bf16[1,256,256]{2,1,0:T(8,128)(2,1)S(1)}, bf16[1,256,256]{2,1,0:T(8,128)(2,1)S(1)}, u32[]{:S(2)}, u32[]{:S(2)}) %collective-permute-start.8) | collective-permute-done | bytes 131104 | tf_op jit(solution)/shard_map/ppermute | solution.py:13
  20.2 0.1 fusion.18
  20.3 2.7 %collective-permute-start.10 = (bf16[256,256]{1,0:T(8,128)(2,1)S(1)}, bf16[256,256]{1,0:T(8,128)(2,1)S(1)}, u32[]{:S(2)}, u32[]{:S(2)}) collective-permute-start(bf16[256,256]{1,0:T(8,128)(2,1)S(1)} %fusion.18), channel_id=1, source_target_pairs={{0,16},{2,18},{4,20},{6,22},{8,24},{10,26},{12,28},{14,30},{16,0},... | collective-permute-start | bytes 393224 | tf_op jit(solution)/shard_map/ppermute | solution.py:13
  23.0 0.0 collective-permute-done.3
  23.0 0.3 collective-permute-done.5
  23.2 4.3 %collective-permute-done.4 = bf16[256,256]{1,0:T(8,128)(2,1)S(1)} collective-permute-done((bf16[256,256]{1,0:T(8,128)(2,1)S(1)}, bf16[256,256]{1,0:T(8,128)(2,1)S(1)}, u32[]{:S(2)}, u32[]{:S(2)}) %collective-permute-start.4) | collective-permute-done | bytes 131104 | tf_op jit(solution)/shard_map/ppermute | solution.py:13
  27.5 1.5 %collective-permute-done.10 = bf16[256,256]{1,0:T(8,128)(2,1)S(1)} collective-permute-done((bf16[256,256]{1,0:T(8,128)(2,1)S(1)}, bf16[256,256]{1,0:T(8,128)(2,1)S(1)}, u32[]{:S(2)}, u32[]{:S(2)}) %collective-permute-start.10) | collective-permute-done | bytes 131104 | tf_op jit(solution)/shard_map/ppermute | solution.py:13
  29.0 0.0 copy-done
  29.0 0.0 copy-done.1
  29.0 0.9 %fusion.4 = bf16[256,256]{1,0:T(8,128)(2,1)} fusion(bf16[256,256]{1,0:T(8,128)(2,1)S(1)} %copy-done, bf16[256,256]{1,0:T(8,128)(2,1)S(1)} %multiply_convert_fusion.1, bf16[256,256]{1,0:T(8,128)(2,1)S(1)} %collective-permute-done.10, bf16[256,256]{1,0:T(8,128)(2,1)S(1)} %collective-permute-done.5, bf16[256,256]{1,0:T(8,128)(2,1)S(1)} %collective-permute-done.4, ...), kind=kOutput, calls=%fused_computation.10 | convolution fusion | flops 34603008 | bytes 1050624 | tf_op jit(solution)/shard_map/dot_general | solution.py:175
  (4 shorter events, 0.1 us)
Async XLA Ops:
  0.0 29.0 %copy-start = (bf16[256,256]{1,0:T(8,128)(2,1)S(1)}, bf16[256,256]{1,0:T(8,128)(2,1)}, u32[]{:S(2)}) copy-start(bf16[256,256]{1,0:T(8,128)(2,1)} %param.12) | copy-start | bytes 393220
  0.0 5.1 %collective-permute-start.1 = (s32[256]{0:T(256)}, s32[256]{0:T(256)S(1)}, u32[]{:S(2)}, u32[]{:S(2)}) collective-permute-start(s32[256]{0:T(256)} %degrees_hbm.1), channel_id=1, source_target_pairs={{1,0},{0,1},{3,2},{2,3},{5,4},{4,5},{7,6},{6,7},{9,8},{8,9},{11,10... | collective-permute-start | bytes 3080 | tf_op jit(solution)/shard_map/ppermute | solution.py:18
  1.5 5.2 %collective-permute-start = (bf16[256,256]{1,0:T(8,128)(2,1)}, bf16[256,256]{1,0:T(8,128)(2,1)S(1)}, u32[]{:S(2)}, u32[]{:S(2)}) collective-permute-start(bf16[256,256]{1,0:T(8,128)(2,1)} %features_hbm.1), channel_id=1, source_target_pairs={{1,0},{0,1},{3,2},{2,3},{5,4},{4,5},{7,6},{6,7},{9,8},{8,9},{11,10... | collective-permute-start | bytes 393224 | tf_op jit(solution)/shard_map/ppermute | solution.py:18
  7.6 1.8 %collective-permute-start.6 = (bf16[3,256,256]{2,1,0:T(8,128)(2,1)S(1)}, bf16[3,256,256]{2,1,0:T(8,128)(2,1)S(1)}, u32[]{:S(2)}, u32[]{:S(2)}) collective-permute-start(bf16[3,256,256]{2,1,0:T(8,128)(2,1)S(1)} %bitcast.31), channel_id=1, source_target_pairs={{0,2},{2,0},{4,6},{6,4},{8,10},{10,8},{12,14},{14,12},{16,18},{18,... | collective-permute-start | bytes 1179656 | tf_op jit(solution)/shard_map/ppermute | solution.py:13
  8.2 4.9 %collective-permute-start.2 = (bf16[5,256,256]{2,1,0:T(8,128)(2,1)S(1)}, bf16[5,256,256]{2,1,0:T(8,128)(2,1)S(1)}, u32[]{:S(2)}, u32[]{:S(2)}) collective-permute-start(bf16[5,256,256]{2,1,0:T(8,128)(2,1)S(1)} %bitcast.34), channel_id=1, source_target_pairs={{0,2},{2,0},{4,6},{6,4},{8,10},{10,8},{12,14},{14,12},{16,18},{18,... | collective-permute-start | bytes 1966088 | tf_op jit(solution)/shard_map/ppermute | solution.py:13
  9.5 6.0 %collective-permute-start.7 = (bf16[1,256,256]{2,1,0:T(8,128)(2,1)S(1)}, bf16[1,256,256]{2,1,0:T(8,128)(2,1)S(1)}, u32[]{:S(2)}, u32[]{:S(2)}) collective-permute-start(bf16[1,256,256]{2,1,0:T(8,128)(2,1)S(1)} %get-tuple-element.20), channel_id=1, source_target_pairs={{0,4},{2,6},{4,0},{6,2},{8,12},{10,14},{12,8},{14,10},{16,20},{18,... | collective-permute-start | bytes 393224 | tf_op jit(solution)/shard_map/ppermute | solution.py:13
  10.1 6.7 %collective-permute-start.9 = (bf16[1,256,256]{2,1,0:T(8,128)(2,1)S(1)}, bf16[1,256,256]{2,1,0:T(8,128)(2,1)S(1)}, u32[]{:S(2)}, u32[]{:S(2)}) collective-permute-start(bf16[1,256,256]{2,1,0:T(8,128)(2,1)S(1)} %get-tuple-element.21), channel_id=1, source_target_pairs={{0,8},{2,10},{4,12},{6,14},{8,0},{10,2},{12,4},{14,6},{16,24},{18,... | collective-permute-start | bytes 393224 | tf_op jit(solution)/shard_map/ppermute | solution.py:13
  11.7 8.5 %collective-permute-start.8 = (bf16[1,256,256]{2,1,0:T(8,128)(2,1)S(1)}, bf16[1,256,256]{2,1,0:T(8,128)(2,1)S(1)}, u32[]{:S(2)}, u32[]{:S(2)}) collective-permute-start(bf16[1,256,256]{2,1,0:T(8,128)(2,1)S(1)} %get-tuple-element.22), channel_id=1, source_target_pairs={{0,12},{2,14},{4,8},{6,10},{8,4},{10,6},{12,0},{14,2},{16,28},{18,... | collective-permute-start | bytes 393224 | tf_op jit(solution)/shard_map/ppermute | solution.py:13
  13.1 16.0 %copy-start.1 = (f32[256]{0:T(256)S(1)}, f32[256]{0:T(256)}, u32[]{:S(2)}) copy-start(f32[256]{0:T(256)} %param.13) | copy-start | bytes 3076
  13.3 9.7 %collective-permute-start.3 = (bf16[256,256]{1,0:T(8,128)(2,1)S(1)}, bf16[256,256]{1,0:T(8,128)(2,1)S(1)}, u32[]{:S(2)}, u32[]{:S(2)}) collective-permute-start(bf16[256,256]{1,0:T(8,128)(2,1)S(1)} %get-tuple-element.17), channel_id=1, source_target_pairs={{0,4},{2,6},{4,0},{6,2},{8,12},{10,14},{12,8},{14,10},{16,20},{18,... | collective-permute-start | bytes 393224 | tf_op jit(solution)/shard_map/ppermute | solution.py:13
  13.9 9.4 %collective-permute-start.5 = (bf16[256,256]{1,0:T(8,128)(2,1)S(1)}, bf16[256,256]{1,0:T(8,128)(2,1)S(1)}, u32[]{:S(2)}, u32[]{:S(2)}) collective-permute-start(bf16[256,256]{1,0:T(8,128)(2,1)S(1)} %get-tuple-element.18), channel_id=1, source_target_pairs={{0,8},{2,10},{4,12},{6,14},{8,0},{10,2},{12,4},{14,6},{16,24},{18,... | collective-permute-start | bytes 393224 | tf_op jit(solution)/shard_map/ppermute | solution.py:13
  15.5 12.1 %collective-permute-start.4 = (bf16[256,256]{1,0:T(8,128)(2,1)S(1)}, bf16[256,256]{1,0:T(8,128)(2,1)S(1)}, u32[]{:S(2)}, u32[]{:S(2)}) collective-permute-start(bf16[256,256]{1,0:T(8,128)(2,1)S(1)} %get-tuple-element.19), channel_id=1, source_target_pairs={{0,12},{2,14},{4,8},{6,10},{8,4},{10,6},{12,0},{14,2},{16,28},{18,... | collective-permute-start | bytes 393224 | tf_op jit(solution)/shard_map/ppermute | solution.py:13
  20.3 8.7 %collective-permute-start.10 = (bf16[256,256]{1,0:T(8,128)(2,1)S(1)}, bf16[256,256]{1,0:T(8,128)(2,1)S(1)}, u32[]{:S(2)}, u32[]{:S(2)}) collective-permute-start(bf16[256,256]{1,0:T(8,128)(2,1)S(1)} %fusion.18), channel_id=1, source_target_pairs={{0,16},{2,18},{4,20},{6,22},{8,24},{10,26},{12,28},{14,30},{16,0},... | collective-permute-start | bytes 393224 | tf_op jit(solution)/shard_map/ppermute | solution.py:13

commit v2 on v1

--- a/solution.py
+++ b/solution.py
@@ -122,9 +122,9 @@
         degrees_in = from_ahead(degrees, "col", step)
         moved.append((features_in, degrees_in))
 
-    first = [h * 8 + q * 2 for q in (1, 2, 3) for h in range(1, high)]
-    rest = [h * 8 for h in range(1, high)] + [q * 2 for q in range(4)]
-    orders = [[delta | other for delta in part] for part in (first, rest) for other in (1, 0)]
+    far = {q: [h * 8 + q * 2 for h in range(1, high)] for q in range(4)}
+    first, second, rest = far[3], far[2] + far[1], far[0] + [q * 2 for q in range(4)]
+    orders = [[delta | other for delta in part] for part in (first, second, rest) for other in (1, 0)]
     *dense, features, degrees = arrange(
         blocks, block_ids, counts, features, degrees, orders, cols * seg_rows
     )
@@ -139,10 +139,11 @@
     def product(matrix, features_in):
         return jnp.dot(matrix, features_in, preferred_element_type=jnp.float32)
 
+    ahead = [lax.optimization_barrier(product(matrix[:, :seg_rows], parts[0])) for matrix in dense[:4]]
+
     def term(at):
-        if at < 2:
-            ahead = lax.optimization_barrier(product(dense[at][:, :seg_rows], parts[0]))
-            total = ahead + product(dense[at][:, seg_rows:], gathered)
+        if at < len(ahead):
+            total = ahead[at] + product(dense[at][:, seg_rows:], gathered)
         else:
             total = product(dense[at], jnp.concatenate(parts, axis=0))
         return narrow(total).reshape(-1, seg_rows, width)
@@ -153,12 +154,14 @@
         kept = term(mine)
         return narrow(add(kept, sent))
 
-    chip_first = over_cores(1, 0).reshape(3, high - 1, seg_rows, width)
+    leaving = {3: over_cores(1, 0)}
+    both = over_cores(3, 2)
+    leaving[2], leaving[1] = both[: high - 1], both[high - 1 :]
     got_far = []
-    for q in (1, 3, 2):
-        got_far.append(swap_with(chip_first[q - 1], "row", 2 * q))
+    for q in (3, 2, 1):
+        got_far.append(swap_with(leaving[q], "row", 2 * q))
 
-    chip_rest = over_cores(3, 2)
+    chip_rest = over_cores(5, 4)
     chip_far, chip_near = chip_rest[: high - 1], chip_rest[high - 1 :]
     quad_far = narrow(add(chip_far, *got_far))
     across = []

time: 30.1 us -> 34 us (1.13)
  the two profiles are of different devices: /device:TPU:2 before, /device:TPU:0 now
where the time goes in v2:
time: 34 us; the launch traced here: 33.8 us
  waiting for transfers between devices  13.6 us (40%)
  starting transfers between devices  13.5 us (40%)
  matrix products  3.55 us (10%)
  Pallas kernels  2.42 us (7%)
  other arithmetic  0.53 us (2%)
    ppermute x10, waiting for transfers between devices, swap_with(): return lax.ppermute(value, axis, [(i, i ^ flip) for i in range(size)])  13.2 us
    ppermute x10, starting transfers between devices, swap_with(): return lax.ppermute(value, axis, [(i, i ^ flip) for i in range(size)])  10.5 us
    ppermute x2, starting transfers between devices, from_ahead(): lax.ppermute(value, axis, [((i + distance) % size, i) for i in range(size)])  3.07 us
    dot_general x10, matrix products, product(): return jnp.dot(matrix, features_in, preferred_element_type=jnp.float32)  2.64 us
    pallas_call x1, Pallas kernels, arrange(): pl.pallas_call(functools.partial(arrange_kernel, orders, geometry), out_s...  2.42 us
    dot_general x1, matrix products, local(): jnp.dot(combined, weight, preferred_element_type=jnp.float32) + out_bias  0.91 us
  transfers between devices with their start and end apart: 12, of which 7 were waited for; matrix products, arithmetic and copies ran while one was open for 8% of the time, Pallas kernels for 7%

profile of v2, /device:TPU:0, one launch (start us, length us, event | category | flops | bytes accessed | tf_op | source)
XLA Modules:
  0.0 33.8 jit_solution(920635015836237473)
XLA Ops:
  0.0 0.0 copy-start
  0.0 3.0 %collective-permute-start = (bf16[256,256]{1,0:T(8,128)(2,1)}, bf16[256,256]{1,0:T(8,128)(2,1)S(1)}, u32[]{:S(2)}, u32[]{:S(2)}) collective-permute-start(bf16[256,256]{1,0:T(8,128)(2,1)} %features_hbm.1), channel_id=1, source_target_pairs={{1,0},{0,1},{3,2},{2,3},{5,4},{4,5},{7,6},{6,7},{9,8},{8,9},{11,10... | collective-permute-start | bytes 393224 | tf_op jit(solution)/shard_map/ppermute | solution.py:18
  3.0 0.1 collective-permute-start.1
  3.1 2.4 %shard_map.73 = (bf16[256,512]{1,0:T(8,128)(2,1)S(1)}, bf16[256,512]{1,0:T(8,128)(2,1)S(1)}, bf16[512,512]{1,0:T(8,128)(2,1)S(1)}, bf16[512,512]{1,0:T(8,128)(2,...) custom-call(s32[8,16]{1,0:T(8,128)} %bitcast.47, ...), custom_call_target="tpu_custom_call" | custom-call | bytes 8388608 | tf_op jit(solution)/shard_map/pallas_call | solution.py:85
  5.5 0.1 multiply_convert_fusion.1
  5.6 0.2 fusion.28
  5.8 0.2 fusion.20
  6.0 0.2 fusion.23
  6.3 0.2 fusion.31
  6.5 0.3 collective-permute-done.1
  6.8 0.0 collective-permute-done
  6.8 0.1 multiply_convert_fusion
  6.9 0.2 fusion.7
  7.1 0.1 collective-permute-start.6
  7.2 0.2 fusion.2
  7.4 0.6 %collective-permute-start.8 = (bf16[2,256,256]{2,1,0:T(8,128)(2,1)S(1)}, bf16[2,256,256]{2,1,0:T(8,128)(2,1)S(1)}, u32[]{:S(2)}, u32[]{:S(2)}) collective-permute-start(bf16[2,256,256]{2,1,0:T(8,128)(2,1)S(1)} %bitcast.46), channel_id=1, source_target_pairs={{0,2},{2,0},{4,6},{6,4},{8,10},{10,8},{12,14},{14,12},{16,18},{18,... | collective-permute-start | bytes 786440 | tf_op jit(solution)/shard_map/ppermute | solution.py:13
  8.0 0.5 %convolution_convert_fusion = bf16[1280,256]{1,0:T(8,128)(2,1)S(1)} fusion(bf16[1280,512]{1,0:T(8,128)(2,1)S(1)} %get-tuple-element.16, bf16[256,256]{1,0:T(8,128)(2,1)S(1)} %multiply_convert_fusion, bf16[256,256]{1,0:T(8,128)(2,1)S(1)} %multiply_convert_fusion.1), kind=kOutput, calls=%fused_computation | convolution fusion | flops 336396288 | bytes 2228224 | tf_op jit(solution)/shard_map/dot_general | solution.py:140
  8.5 0.1 collective-permute-start.2
  8.6 0.5 %convolution_convert_fusion.1 = bf16[1280,256]{1,0:T(8,128)(2,1)S(1)} fusion(bf16[1280,512]{1,0:T(8,128)(2,1)S(1)} %get-tuple-element.14, bf16[256,256]{1,0:T(8,128)(2,1)S(1)} %multiply_convert_fusion, bf16[256,256]{1,0:T(8,128)(2,1)S(1)} %multiply_convert_fusion.1), kind=kOutput, calls=%fused_computation.1 | convolution fusion | flops 336396288 | bytes 2228224 | tf_op jit(solution)/shard_map/dot_general | solution.py:140
  9.1 0.2 fusion.1
  9.3 0.0 collective-permute-done.6
  9.3 0.2 fusion.11
  9.5 2.8 %collective-permute-start.7 = (bf16[1,256,256]{2,1,0:T(8,128)(2,1)S(1)}, bf16[1,256,256]{2,1,0:T(8,128)(2,1)S(1)}, u32[]{:S(2)}, u32[]{:S(2)}) collective-permute-start(bf16[1,256,256]{2,1,0:T(8,128)(2,1)S(1)} %fusion.11), channel_id=1, source_target_pairs={{0,12},{2,14},{4,8},{6,10},{8,4},{10,6},{12,0},{14,2},{16,28},{18,... | collective-permute-start | bytes 393224 | tf_op jit(solution)/shard_map/ppermute | solution.py:13
  12.3 0.0 collective-permute-done.8
  12.3 0.1 fusion.12
  12.4 0.6 %collective-permute-start.10 = (bf16[1,256,256]{2,1,0:T(8,128)(2,1)S(1)}, bf16[1,256,256]{2,1,0:T(8,128)(2,1)S(1)}, u32[]{:S(2)}, u32[]{:S(2)}) collective-permute-start(bf16[1,256,256]{2,1,0:T(8,128)(2,1)S(1)} %get-tuple-element.25), channel_id=1, source_target_pairs={{0,4},{2,6},{4,0},{6,2},{8,12},{10,14},{12,8},{14,10},{16,20},{18,... | collective-permute-start | bytes 393224 | tf_op jit(solution)/shard_map/ppermute | solution.py:13
  13.0 0.2 collective-permute-start.9
  13.2 0.0 collective-permute-done.2
  13.2 0.0 copy-start.1
  13.2 0.2 fusion
  13.4 3.1 %collective-permute-done.7 = bf16[1,256,256]{2,1,0:T(8,128)(2,1)S(1)} collective-permute-done((bf16[1,256,256]{2,1,0:T(8,128)(2,1)S(1)}, bf16[1,256,256]{2,1,0:T(8,128)(2,1)S(1)}, u32[]{:S(2)}, u32[]{:S(2)}) %collective-permute-start.7) | collective-permute-done | bytes 131104 | tf_op jit(solution)/shard_map/ppermute | solution.py:13
  16.5 2.7 %collective-permute-done.10 = bf16[1,256,256]{2,1,0:T(8,128)(2,1)S(1)} collective-permute-done((bf16[1,256,256]{2,1,0:T(8,128)(2,1)S(1)}, bf16[1,256,256]{2,1,0:T(8,128)(2,1)S(1)}, u32[]{:S(2)}, u32[]{:S(2)}) %collective-permute-start.10) | collective-permute-done | bytes 131104 | tf_op jit(solution)/shard_map/ppermute | solution.py:13
  19.2 0.2 collective-permute-done.9
  19.4 0.1 fusion.25
  19.5 2.7 %collective-permute-start.11 = (bf16[256,256]{1,0:T(8,128)(2,1)S(1)}, bf16[256,256]{1,0:T(8,128)(2,1)S(1)}, u32[]{:S(2)}, u32[]{:S(2)}) collective-permute-start(bf16[256,256]{1,0:T(8,128)(2,1)S(1)} %fusion.25), channel_id=1, source_target_pairs={{0,16},{2,18},{4,20},{6,22},{8,24},{10,26},{12,28},{14,30},{16,0},... | collective-permute-start | bytes 393224 | tf_op jit(solution)/shard_map/ppermute | solution.py:13
  22.2 1.4 %collective-permute-start.3 = (bf16[256,256]{1,0:T(8,128)(2,1)S(1)}, bf16[256,256]{1,0:T(8,128)(2,1)S(1)}, u32[]{:S(2)}, u32[]{:S(2)}) collective-permute-start(bf16[256,256]{1,0:T(8,128)(2,1)S(1)} %get-tuple-element.21), channel_id=1, source_target_pairs={{0,4},{2,6},{4,0},{6,2},{8,12},{10,14},{12,8},{14,10},{16,20},{18,... | collective-permute-start | bytes 393224 | tf_op jit(solution)/shard_map/ppermute | solution.py:13
  23.6 1.6 %collective-permute-start.4 = (bf16[256,256]{1,0:T(8,128)(2,1)S(1)}, bf16[256,256]{1,0:T(8,128)(2,1)S(1)}, u32[]{:S(2)}, u32[]{:S(2)}) collective-permute-start(bf16[256,256]{1,0:T(8,128)(2,1)S(1)} %get-tuple-element.23), channel_id=1, source_target_pairs={{0,12},{2,14},{4,8},{6,10},{8,4},{10,6},{12,0},{14,2},{16,28},{18,... | collective-permute-start | bytes 393224 | tf_op jit(solution)/shard_map/ppermute | solution.py:13
  25.2 0.4 %collective-permute-start.5 = (bf16[256,256]{1,0:T(8,128)(2,1)S(1)}, bf16[256,256]{1,0:T(8,128)(2,1)S(1)}, u32[]{:S(2)}, u32[]{:S(2)}) collective-permute-start(bf16[256,256]{1,0:T(8,128)(2,1)S(1)} %get-tuple-element.22), channel_id=1, source_target_pairs={{0,8},{2,10},{4,12},{6,14},{8,0},{10,2},{12,4},{14,6},{16,24},{18,... | collective-permute-start | bytes 393224 | tf_op jit(solution)/shard_map/ppermute | solution.py:13
  25.7 3.1 %collective-permute-done.11 = bf16[256,256]{1,0:T(8,128)(2,1)S(1)} collective-permute-done((bf16[256,256]{1,0:T(8,128)(2,1)S(1)}, bf16[256,256]{1,0:T(8,128)(2,1)S(1)}, u32[]{:S(2)}, u32[]{:S(2)}) %collective-permute-start.11) | collective-permute-done | bytes 131104 | tf_op jit(solution)/shard_map/ppermute | solution.py:13
  28.7 0.0 collective-permute-done.3
  28.7 3.5 %collective-permute-done.4 = bf16[256,256]{1,0:T(8,128)(2,1)S(1)} collective-permute-done((bf16[256,256]{1,0:T(8,128)(2,1)S(1)}, bf16[256,256]{1,0:T(8,128)(2,1)S(1)}, u32[]{:S(2)}, u32[]{:S(2)}) %collective-permute-start.4) | collective-permute-done | bytes 131104 | tf_op jit(solution)/shard_map/ppermute | solution.py:13
  32.3 0.6 %collective-permute-done.5 = bf16[256,256]{1,0:T(8,128)(2,1)S(1)} collective-permute-done((bf16[256,256]{1,0:T(8,128)(2,1)S(1)}, bf16[256,256]{1,0:T(8,128)(2,1)S(1)}, u32[]{:S(2)}, u32[]{:S(2)}) %collective-permute-start.5) | collective-permute-done | bytes 131104 | tf_op jit(solution)/shard_map/ppermute | solution.py:13
  32.9 0.0 copy-done
  32.9 0.0 copy-done.1
  32.9 0.9 %fusion.6 = bf16[256,256]{1,0:T(8,128)(2,1)} fusion(bf16[256,256]{1,0:T(8,128)(2,1)S(1)} %copy-done, bf16[256,256]{1,0:T(8,128)(2,1)S(1)} %multiply_convert_fusion.1, bf16[256,256]{1,0:T(8,128)(2,1)S(1)} %collective-permute-done.11, bf16[256,256]{1,0:T(8,128)(2,1)S(1)} %collective-permute-done.5, bf16[256,256]{1,0:T(8,128)(2,1)S(1)} %collective-permute-done.4, ...), kind=kOutput, calls=%fused_computation.14 | convolution fusion | flops 34603008 | bytes 1050624 | tf_op jit(solution)/shard_map/dot_general | solution.py:178
  (4 shorter events, 0.1 us)
Async XLA Ops:
  0.0 32.9 %copy-start = (bf16[256,256]{1,0:T(8,128)(2,1)S(1)}, bf16[256,256]{1,0:T(8,128)(2,1)}, u32[]{:S(2)}) copy-start(bf16[256,256]{1,0:T(8,128)(2,1)} %param.12) | copy-start | bytes 393220
  0.0 6.8 %collective-permute-start = (bf16[256,256]{1,0:T(8,128)(2,1)}, bf16[256,256]{1,0:T(8,128)(2,1)S(1)}, u32[]{:S(2)}, u32[]{:S(2)}) collective-permute-start(bf16[256,256]{1,0:T(8,128)(2,1)} %features_hbm.1), channel_id=1, source_target_pairs={{1,0},{0,1},{3,2},{2,3},{5,4},{4,5},{7,6},{6,7},{9,8},{8,9},{11,10... | collective-permute-start | bytes 393224 | tf_op jit(solution)/shard_map/ppermute | solution.py:18
  3.0 3.8 %collective-permute-start.1 = (s32[256]{0:T(256)}, s32[256]{0:T(256)S(1)}, u32[]{:S(2)}, u32[]{:S(2)}) collective-permute-start(s32[256]{0:T(256)} %degrees_hbm.1), channel_id=1, source_target_pairs={{1,0},{0,1},{3,2},{2,3},{5,4},{4,5},{7,6},{6,7},{9,8},{8,9},{11,10... | collective-permute-start | bytes 3080 | tf_op jit(solution)/shard_map/ppermute | solution.py:18
  7.1 2.2 %collective-permute-start.6 = (bf16[1,256,256]{2,1,0:T(8,128)(2,1)S(1)}, bf16[1,256,256]{2,1,0:T(8,128)(2,1)S(1)}, u32[]{:S(2)}, u32[]{:S(2)}) collective-permute-start(bf16[1,256,256]{2,1,0:T(8,128)(2,1)S(1)} %fusion.7), channel_id=1, source_target_pairs={{0,2},{2,0},{4,6},{6,4},{8,10},{10,8},{12,14},{14,12},{16,18},{18,... | collective-permute-start | bytes 393224 | tf_op jit(solution)/shard_map/ppermute | solution.py:13
  7.4 4.9 %collective-permute-start.8 = (bf16[2,256,256]{2,1,0:T(8,128)(2,1)S(1)}, bf16[2,256,256]{2,1,0:T(8,128)(2,1)S(1)}, u32[]{:S(2)}, u32[]{:S(2)}) collective-permute-start(bf16[2,256,256]{2,1,0:T(8,128)(2,1)S(1)} %bitcast.46), channel_id=1, source_target_pairs={{0,2},{2,0},{4,6},{6,4},{8,10},{10,8},{12,14},{14,12},{16,18},{18,... | collective-permute-start | bytes 786440 | tf_op jit(solution)/shard_map/ppermute | solution.py:13
  8.5 4.8 %collective-permute-start.2 = (bf16[5,256,256]{2,1,0:T(8,128)(2,1)S(1)}, bf16[5,256,256]{2,1,0:T(8,128)(2,1)S(1)}, u32[]{:S(2)}, u32[]{:S(2)}) collective-permute-start(bf16[5,256,256]{2,1,0:T(8,128)(2,1)S(1)} %bitcast.49), channel_id=1, source_target_pairs={{0,2},{2,0},{4,6},{6,4},{8,10},{10,8},{12,14},{14,12},{16,18},{18,... | collective-permute-start | bytes 1966088 | tf_op jit(solution)/shard_map/ppermute | solution.py:13
  9.5 7.0 %collective-permute-start.7 = (bf16[1,256,256]{2,1,0:T(8,128)(2,1)S(1)}, bf16[1,256,256]{2,1,0:T(8,128)(2,1)S(1)}, u32[]{:S(2)}, u32[]{:S(2)}) collective-permute-start(bf16[1,256,256]{2,1,0:T(8,128)(2,1)S(1)} %fusion.11), channel_id=1, source_target_pairs={{0,12},{2,14},{4,8},{6,10},{8,4},{10,6},{12,0},{14,2},{16,28},{18,... | collective-permute-start | bytes 393224 | tf_op jit(solution)/shard_map/ppermute | solution.py:13
  12.4 6.9 %collective-permute-start.10 = (bf16[1,256,256]{2,1,0:T(8,128)(2,1)S(1)}, bf16[1,256,256]{2,1,0:T(8,128)(2,1)S(1)}, u32[]{:S(2)}, u32[]{:S(2)}) collective-permute-start(bf16[1,256,256]{2,1,0:T(8,128)(2,1)S(1)} %get-tuple-element.25), channel_id=1, source_target_pairs={{0,4},{2,6},{4,0},{6,2},{8,12},{10,14},{12,8},{14,10},{16,20},{18,... | collective-permute-start | bytes 393224 | tf_op jit(solution)/shard_map/ppermute | solution.py:13
  13.0 6.5 %collective-permute-start.9 = (bf16[1,256,256]{2,1,0:T(8,128)(2,1)S(1)}, bf16[1,256,256]{2,1,0:T(8,128)(2,1)S(1)}, u32[]{:S(2)}, u32[]{:S(2)}) collective-permute-start(bf16[1,256,256]{2,1,0:T(8,128)(2,1)S(1)} %get-tuple-element.24), channel_id=1, source_target_pairs={{0,8},{2,10},{4,12},{6,14},{8,0},{10,2},{12,4},{14,6},{16,24},{18,... | collective-permute-start | bytes 393224 | tf_op jit(solution)/shard_map/ppermute | solution.py:13
  13.2 19.7 %copy-start.1 = (f32[256]{0:T(256)S(1)}, f32[256]{0:T(256)}, u32[]{:S(2)}) copy-start(f32[256]{0:T(256)} %param.13) | copy-start | bytes 3076
  19.5 9.2 %collective-permute-start.11 = (bf16[256,256]{1,0:T(8,128)(2,1)S(1)}, bf16[256,256]{1,0:T(8,128)(2,1)S(1)}, u32[]{:S(2)}, u32[]{:S(2)}) collective-permute-start(bf16[256,256]{1,0:T(8,128)(2,1)S(1)} %fusion.25), channel_id=1, source_target_pairs={{0,16},{2,18},{4,20},{6,22},{8,24},{10,26},{12,28},{14,30},{16,0},... | collective-permute-start | bytes 393224 | tf_op jit(solution)/shard_map/ppermute | solution.py:13
  22.2 6.6 %collective-permute-start.3 = (bf16[256,256]{1,0:T(8,128)(2,1)S(1)}, bf16[256,256]{1,0:T(8,128)(2,1)S(1)}, u32[]{:S(2)}, u32[]{:S(2)}) collective-permute-start(bf16[256,256]{1,0:T(8,128)(2,1)S(1)} %get-tuple-element.21), channel_id=1, source_target_pairs={{0,4},{2,6},{4,0},{6,2},{8,12},{10,14},{12,8},{14,10},{16,20},{18,... | collective-permute-start | bytes 393224 | tf_op jit(solution)/shard_map/ppermute | solution.py:13
  23.6 8.6 %collective-permute-start.4 = (bf16[256,256]{1,0:T(8,128)(2,1)S(1)}, bf16[256,256]{1,0:T(8,128)(2,1)S(1)}, u32[]{:S(2)}, u32[]{:S(2)}) collective-permute-start(bf16[256,256]{1,0:T(8,128)(2,1)S(1)} %get-tuple-element.23), channel_id=1, source_target_pairs={{0,12},{2,14},{4,8},{6,10},{8,4},{10,6},{12,0},{14,2},{16,28},{18,... | collective-permute-start | bytes 393224 | tf_op jit(solution)/shard_map/ppermute | solution.py:13
  25.2 7.7 %collective-permute-start.5 = (bf16[256,256]{1,0:T(8,128)(2,1)S(1)}, bf16[256,256]{1,0:T(8,128)(2,1)S(1)}, u32[]{:S(2)}, u32[]{:S(2)}) collective-permute-start(bf16[256,256]{1,0:T(8,128)(2,1)S(1)} %get-tuple-element.22), channel_id=1, source_target_pairs={{0,8},{2,10},{4,12},{6,14},{8,0},{10,2},{12,4},{14,6},{16,24},{18,... | collective-permute-start | bytes 393224 | tf_op jit(solution)/shard_map/ppermute | solution.py:13

commit v3 on v2

--- a/solution.py
+++ b/solution.py
@@ -123,8 +123,8 @@
         moved.append((features_in, degrees_in))
 
     far = {q: [h * 8 + q * 2 for h in range(1, high)] for q in range(4)}
-    first, second, rest = far[3], far[2] + far[1], far[0] + [q * 2 for q in range(4)]
-    orders = [[delta | other for delta in part] for part in (first, second, rest) for other in (1, 0)]
+    first, second = far[3], far[2] + far[1] + far[0] + [q * 2 for q in range(4)]
+    orders = [[delta | other for delta in part] for part in (first, second) for other in (1, 0)]
     *dense, features, degrees = arrange(
         blocks, block_ids, counts, features, degrees, orders, cols * seg_rows
     )
@@ -139,7 +139,7 @@
     def product(matrix, features_in):
         return jnp.dot(matrix, features_in, preferred_element_type=jnp.float32)
 
-    ahead = [lax.optimization_barrier(product(matrix[:, :seg_rows], parts[0])) for matrix in dense[:4]]
+    ahead = [lax.optimization_barrier(product(matrix[:, :seg_rows], parts[0])) for matrix in dense[:2]]
 
     def term(at):
         if at < len(ahead):
@@ -156,13 +156,13 @@
 
     leaving = {3: over_cores(1, 0)}
     both = over_cores(3, 2)
-    leaving[2], leaving[1] = both[: high - 1], both[high - 1 :]
+    count = high - 1
+    leaving[2], leaving[1] = both[:count], both[count : 2 * count]
+    chip_far, chip_near = both[2 * count : 3 * count], both[3 * count :]
     got_far = []
     for q in (3, 2, 1):
         got_far.append(swap_with(leaving[q], "row", 2 * q))
 
-    chip_rest = over_cores(5, 4)
-    chip_far, chip_near = chip_rest[: high - 1], chip_rest[high - 1 :]
     quad_far = narrow(add(chip_far, *got_far))
     across = []
     for h in range(1, high):

time: 34 us -> 32.6 us (0.959)
  waiting for transfers between devices: 13.6 us -> 11.4 us
  starting transfers between devices: 13.5 us -> 15 us
  matrix products: 3.55 us -> 2.93 us
    ppermute x10 -> x9, waiting for transfers between devices: 13.2 us -> 10.2 us  [swap_with(): return lax.ppermute(value, axis, [(i, i ^ flip) for i in range(size)])]
    ppermute x10 -> x9, starting transfers between devices: 10.5 us -> 12 us  [swap_with(): return lax.ppermute(value, axis, [(i, i ^ flip) for i in range(size)])]
    ppermute x2, waiting for transfers between devices: 0.33 us -> 1.17 us  [from_ahead(): lax.ppermute(value, axis, [((i + distance) % size, i) for i in range(size)])]
    dot_general x10 -> x6, matrix products: 2.64 us -> 2.02 us  [product(): return jnp.dot(matrix, features_in, preferred_element_type=jnp.float32)]
  transfers between devices with their start and end apart: 12 -> 11, of which waited for: 7 -> 7; matrix products, arithmetic and copies ran while one was open for 8% -> 6% of each run, Pallas kernels for 7% -> 7%
where the time goes in v3:
time: 32.6 us; the launch traced here: 32.5 us
  starting transfers between devices  15 us (46%)
  waiting for transfers between devices  11.4 us (35%)
  matrix products  2.93 us (9%)
  Pallas kernels  2.42 us (7%)
  other arithmetic  0.54 us (2%)
    ppermute x9, starting transfers between devices, swap_with(): return lax.ppermute(value, axis, [(i, i ^ flip) for i in range(size)])  12 us
    ppermute x9, waiting for transfers between devices, swap_with(): return lax.ppermute(value, axis, [(i, i ^ flip) for i in range(size)])  10.2 us
    ppermute x2, starting transfers between devices, from_ahead(): lax.ppermute(value, axis, [((i + distance) % size, i) for i in range(size)])  3.07 us
    pallas_call x1, Pallas kernels, arrange(): pl.pallas_call(functools.partial(arrange_kernel, orders, geometry), out_s...  2.42 us
    dot_general x6, matrix products, product(): return jnp.dot(matrix, features_in, preferred_element_type=jnp.float32)  2.02 us
    ppermute x2, waiting for transfers between devices, from_ahead(): lax.ppermute(value, axis, [((i + distance) % size, i) for i in range(size)])  1.17 us
    dot_general x1, matrix products, local(): jnp.dot(combined, weight, preferred_element_type=jnp.float32) + out_bias  0.91 us
  transfers between devices with their start and end apart: 11, of which 7 were waited for; matrix products, arithmetic and copies ran while one was open for 6% of the time, Pallas kernels for 7%

profile of v3, /device:TPU:0, one launch (start us, length us, event | category | flops | bytes accessed | tf_op | source)
XLA Modules:
  0.0 32.5 jit_solution(3990451850020078763)
XLA Ops:
  0.0 0.0 copy-start
  0.0 3.0 %collective-permute-start = (bf16[256,256]{1,0:T(8,128)(2,1)}, bf16[256,256]{1,0:T(8,128)(2,1)S(1)}, u32[]{:S(2)}, u32[]{:S(2)}) collective-permute-start(bf16[256,256]{1,0:T(8,128)(2,1)} %features_hbm.1), channel_id=1, source_target_pairs={{1,0},{0,1},{3,2},{2,3},{5,4},{4,5},{7,6},{6,7},{9,8},{8,9},{11,10... | collective-permute-start | bytes 393224 | tf_op jit(solution)/shard_map/ppermute | solution.py:18
  3.0 0.1 collective-permute-start.1
  3.1 2.4 %shard_map.73 = (bf16[256,512]{1,0:T(8,128)(2,1)S(1)}, bf16[256,512]{1,0:T(8,128)(2,1)S(1)}, bf16[1792,512]{1,0:T(8,128)(2,1)S(1)}, bf16[1792,512]{1,0:T(8,128)(...) custom-call(s32[8,16]{1,0:T(8,128)} %bitcast.38, s32[1,16]{1,0:T(1,128)} %bitcast.39, ...), custom_call_target="tpu_custom_call" | custom-call | bytes 8388608 | tf_op jit(solution)/shard_map/pallas_call | solution.py:85
  5.5 0.1 multiply_convert_fusion.1
  5.6 1.2 %collective-permute-done.1 = s32[256]{0:T(256)S(1)} collective-permute-done((s32[256]{0:T(256)}, s32[256]{0:T(256)S(1)}, u32[]{:S(2)}, u32[]{:S(2)}) %collective-permute-start.1) | collective-permute-done | bytes 1056 | tf_op jit(solution)/shard_map/ppermute | solution.py:18
  6.8 0.0 collective-permute-done
  6.8 0.1 multiply_convert_fusion
  6.9 0.6 %convolution_convert_fusion = bf16[1792,256]{1,0:T(8,128)(2,1)S(1)} fusion(bf16[1792,512]{1,0:T(8,128)(2,1)S(1)} %get-tuple-element.14, bf16[256,256]{1,0:T(8,128)(2,1)S(1)} %multiply_convert_fusion, bf16[256,256]{1,0:T(8,128)(2,1)S(1)} %multiply_convert_fusion.1), kind=kOutput, calls=%fused_computation | convolution fusion | flops 470745088 | bytes 3014656 | tf_op jit(solution)/shard_map/dot_general | solution.py:140
  7.5 0.1 collective-permute-start.2
  7.6 0.2 fusion.19
  7.8 0.2 fusion.22
  8.0 0.2 fusion.5
  8.2 0.6 %collective-permute-start.6 = (bf16[1,256,256]{2,1,0:T(8,128)(2,1)S(1)}, bf16[1,256,256]{2,1,0:T(8,128)(2,1)S(1)}, u32[]{:S(2)}, u32[]{:S(2)}) collective-permute-start(bf16[1,256,256]{2,1,0:T(8,128)(2,1)S(1)} %fusion.5), channel_id=1, source_target_pairs={{0,2},{2,0},{4,6},{6,4},{8,10},{10,8},{12,14},{14,12},{16,18},{18,... | collective-permute-start | bytes 393224 | tf_op jit(solution)/shard_map/ppermute | solution.py:13
  8.8 0.6 %convolution_convert_fusion.1 = bf16[1792,256]{1,0:T(8,128)(2,1)S(1)} fusion(bf16[1792,512]{1,0:T(8,128)(2,1)S(1)} %get-tuple-element.12, bf16[256,256]{1,0:T(8,128)(2,1)S(1)} %multiply_convert_fusion, bf16[256,256]{1,0:T(8,128)(2,1)S(1)} %multiply_convert_fusion.1), kind=kOutput, calls=%fused_computation.1 | convolution fusion | flops 470745088 | bytes 3014656 | tf_op jit(solution)/shard_map/dot_general | solution.py:140
  9.4 0.9 %collective-permute-done.6 = bf16[1,256,256]{2,1,0:T(8,128)(2,1)S(1)} collective-permute-done((bf16[1,256,256]{2,1,0:T(8,128)(2,1)S(1)}, bf16[1,256,256]{2,1,0:T(8,128)(2,1)S(1)}, u32[]{:S(2)}, u32[]{:S(2)}) %collective-permute-start.6) | collective-permute-done | bytes 131104 | tf_op jit(solution)/shard_map/ppermute | solution.py:13
  10.3 0.2 fusion.9
  10.5 2.8 %collective-permute-start.7 = (bf16[1,256,256]{2,1,0:T(8,128)(2,1)S(1)}, bf16[1,256,256]{2,1,0:T(8,128)(2,1)S(1)}, u32[]{:S(2)}, u32[]{:S(2)}) collective-permute-start(bf16[1,256,256]{2,1,0:T(8,128)(2,1)S(1)} %fusion.9), channel_id=1, source_target_pairs={{0,12},{2,14},{4,8},{6,10},{8,4},{10,6},{12,0},{14,2},{16,28},{18,... | collective-permute-start | bytes 393224 | tf_op jit(solution)/shard_map/ppermute | solution.py:13
  13.3 0.0 collective-permute-done.2
  13.3 0.0 copy-start.1
  13.3 0.3 fusion
  13.6 0.5 %collective-permute-start.8 = (bf16[1,256,256]{2,1,0:T(8,128)(2,1)S(1)}, bf16[1,256,256]{2,1,0:T(8,128)(2,1)S(1)}, u32[]{:S(2)}, u32[]{:S(2)}) collective-permute-start(bf16[1,256,256]{2,1,0:T(8,128)(2,1)S(1)} %get-tuple-element.19), channel_id=1, source_target_pairs={{0,8},{2,10},{4,12},{6,14},{8,0},{10,2},{12,4},{14,6},{16,24},{18,... | collective-permute-start | bytes 393224 | tf_op jit(solution)/shard_map/ppermute | solution.py:13
  14.1 0.3 collective-permute-start.9
  14.4 1.7 %collective-permute-start.3 = (bf16[256,256]{1,0:T(8,128)(2,1)S(1)}, bf16[256,256]{1,0:T(8,128)(2,1)S(1)}, u32[]{:S(2)}, u32[]{:S(2)}) collective-permute-start(bf16[256,256]{1,0:T(8,128)(2,1)S(1)} %get-tuple-element.17), channel_id=1, source_target_pairs={{0,4},{2,6},{4,0},{6,2},{8,12},{10,14},{12,8},{14,10},{16,20},{18,... | collective-permute-start | bytes 393224 | tf_op jit(solution)/shard_map/ppermute | solution.py:13
  16.1 1.6 %collective-permute-start.4 = (bf16[256,256]{1,0:T(8,128)(2,1)S(1)}, bf16[256,256]{1,0:T(8,128)(2,1)S(1)}, u32[]{:S(2)}, u32[]{:S(2)}) collective-permute-start(bf16[256,256]{1,0:T(8,128)(2,1)S(1)} %get-tuple-element.21), channel_id=1, source_target_pairs={{0,12},{2,14},{4,8},{6,10},{8,4},{10,6},{12,0},{14,2},{16,28},{18,... | collective-permute-start | bytes 393224 | tf_op jit(solution)/shard_map/ppermute | solution.py:13
  17.7 0.1 collective-permute-done.7
  17.8 1.8 %collective-permute-start.5 = (bf16[256,256]{1,0:T(8,128)(2,1)S(1)}, bf16[256,256]{1,0:T(8,128)(2,1)S(1)}, u32[]{:S(2)}, u32[]{:S(2)}) collective-permute-start(bf16[256,256]{1,0:T(8,128)(2,1)S(1)} %get-tuple-element.20), channel_id=1, source_target_pairs={{0,8},{2,10},{4,12},{6,14},{8,0},{10,2},{12,4},{14,6},{16,24},{18,... | collective-permute-start | bytes 393224 | tf_op jit(solution)/shard_map/ppermute | solution.py:13
  19.6 1.3 %collective-permute-done.8 = bf16[1,256,256]{2,1,0:T(8,128)(2,1)S(1)} collective-permute-done((bf16[1,256,256]{2,1,0:T(8,128)(2,1)S(1)}, bf16[1,256,256]{2,1,0:T(8,128)(2,1)S(1)}, u32[]{:S(2)}, u32[]{:S(2)}) %collective-permute-start.8) | collective-permute-done | bytes 131104 | tf_op jit(solution)/shard_map/ppermute | solution.py:13
  20.8 2.4 %collective-permute-done.9 = bf16[1,256,256]{2,1,0:T(8,128)(2,1)S(1)} collective-permute-done((bf16[1,256,256]{2,1,0:T(8,128)(2,1)S(1)}, bf16[1,256,256]{2,1,0:T(8,128)(2,1)S(1)}, u32[]{:S(2)}, u32[]{:S(2)}) %collective-permute-start.9) | collective-permute-done | bytes 131104 | tf_op jit(solution)/shard_map/ppermute | solution.py:13
  23.2 0.1 fusion.16
  23.3 2.7 %collective-permute-start.10 = (bf16[256,256]{1,0:T(8,128)(2,1)S(1)}, bf16[256,256]{1,0:T(8,128)(2,1)S(1)}, u32[]{:S(2)}, u32[]{:S(2)}) collective-permute-start(bf16[256,256]{1,0:T(8,128)(2,1)S(1)} %fusion.16), channel_id=1, source_target_pairs={{0,16},{2,18},{4,20},{6,22},{8,24},{10,26},{12,28},{14,30},{16,0},... | collective-permute-start | bytes 393224 | tf_op jit(solution)/shard_map/ppermute | solution.py:13
  25.9 0.0 collective-permute-done.3
  25.9 0.0 collective-permute-done.4
  25.9 1.1 %collective-permute-done.5 = bf16[256,256]{1,0:T(8,128)(2,1)S(1)} collective-permute-done((bf16[256,256]{1,0:T(8,128)(2,1)S(1)}, bf16[256,256]{1,0:T(8,128)(2,1)S(1)}, u32[]{:S(2)}, u32[]{:S(2)}) %collective-permute-start.5) | collective-permute-done | bytes 131104 | tf_op jit(solution)/shard_map/ppermute | solution.py:13
  27.1 4.5 %collective-permute-done.10 = bf16[256,256]{1,0:T(8,128)(2,1)S(1)} collective-permute-done((bf16[256,256]{1,0:T(8,128)(2,1)S(1)}, bf16[256,256]{1,0:T(8,128)(2,1)S(1)}, u32[]{:S(2)}, u32[]{:S(2)}) %collective-permute-start.10) | collective-permute-done | bytes 131104 | tf_op jit(solution)/shard_map/ppermute | solution.py:13
  31.6 0.0 copy-done
  31.6 0.0 copy-done.1
  31.6 0.9 %fusion.4 = bf16[256,256]{1,0:T(8,128)(2,1)} fusion(bf16[256,256]{1,0:T(8,128)(2,1)S(1)} %copy-done, bf16[256,256]{1,0:T(8,128)(2,1)S(1)} %multiply_convert_fusion.1, bf16[256,256]{1,0:T(8,128)(2,1)S(1)} %collective-permute-done.10, bf16[256,256]{1,0:T(8,128)(2,1)S(1)} %collective-permute-done.5, bf16[256,256]{1,0:T(8,128)(2,1)S(1)} %collective-permute-done.4, ...), kind=kOutput, calls=%fused_computation.10 | convolution fusion | flops 34603008 | bytes 1050624 | tf_op jit(solution)/shard_map/dot_general | solution.py:178
  (3 shorter events, 0.1 us)
Async XLA Ops:
  0.0 31.6 %copy-start = (bf16[256,256]{1,0:T(8,128)(2,1)S(1)}, bf16[256,256]{1,0:T(8,128)(2,1)}, u32[]{:S(2)}) copy-start(bf16[256,256]{1,0:T(8,128)(2,1)} %param.12) | copy-start | bytes 393220
  0.0 6.8 %collective-permute-start = (bf16[256,256]{1,0:T(8,128)(2,1)}, bf16[256,256]{1,0:T(8,128)(2,1)S(1)}, u32[]{:S(2)}, u32[]{:S(2)}) collective-permute-start(bf16[256,256]{1,0:T(8,128)(2,1)} %features_hbm.1), channel_id=1, source_target_pairs={{1,0},{0,1},{3,2},{2,3},{5,4},{4,5},{7,6},{6,7},{9,8},{8,9},{11,10... | collective-permute-start | bytes 393224 | tf_op jit(solution)/shard_map/ppermute | solution.py:18
  3.0 3.8 %collective-permute-start.1 = (s32[256]{0:T(256)}, s32[256]{0:T(256)S(1)}, u32[]{:S(2)}, u32[]{:S(2)}) collective-permute-start(s32[256]{0:T(256)} %degrees_hbm.1), channel_id=1, source_target_pairs={{1,0},{0,1},{3,2},{2,3},{5,4},{4,5},{7,6},{6,7},{9,8},{8,9},{11,10... | collective-permute-start | bytes 3080 | tf_op jit(solution)/shard_map/ppermute | solution.py:18
  7.5 5.7 %collective-permute-start.2 = (bf16[7,256,256]{2,1,0:T(8,128)(2,1)S(1)}, bf16[7,256,256]{2,1,0:T(8,128)(2,1)S(1)}, u32[]{:S(2)}, u32[]{:S(2)}) collective-permute-start(bf16[7,256,256]{2,1,0:T(8,128)(2,1)S(1)} %bitcast.40), channel_id=1, source_target_pairs={{0,2},{2,0},{4,6},{6,4},{8,10},{10,8},{12,14},{14,12},{16,18},{18,... | collective-permute-start | bytes 2752520 | tf_op jit(solution)/shard_map/ppermute | solution.py:13
  8.2 2.1 %collective-permute-start.6 = (bf16[1,256,256]{2,1,0:T(8,128)(2,1)S(1)}, bf16[1,256,256]{2,1,0:T(8,128)(2,1)S(1)}, u32[]{:S(2)}, u32[]{:S(2)}) collective-permute-start(bf16[1,256,256]{2,1,0:T(8,128)(2,1)S(1)} %fusion.5), channel_id=1, source_target_pairs={{0,2},{2,0},{4,6},{6,4},{8,10},{10,8},{12,14},{14,12},{16,18},{18,... | collective-permute-start | bytes 393224 | tf_op jit(solution)/shard_map/ppermute | solution.py:13
  10.5 7.3 %collective-permute-start.7 = (bf16[1,256,256]{2,1,0:T(8,128)(2,1)S(1)}, bf16[1,256,256]{2,1,0:T(8,128)(2,1)S(1)}, u32[]{:S(2)}, u32[]{:S(2)}) collective-permute-start(bf16[1,256,256]{2,1,0:T(8,128)(2,1)S(1)} %fusion.9), channel_id=1, source_target_pairs={{0,12},{2,14},{4,8},{6,10},{8,4},{10,6},{12,0},{14,2},{16,28},{18,... | collective-permute-start | bytes 393224 | tf_op jit(solution)/shard_map/ppermute | solution.py:13
  13.3 18.3 %copy-start.1 = (f32[256]{0:T(256)S(1)}, f32[256]{0:T(256)}, u32[]{:S(2)}) copy-start(f32[256]{0:T(256)} %param.13) | copy-start | bytes 3076
  13.6 7.3 %collective-permute-start.8 = (bf16[1,256,256]{2,1,0:T(8,128)(2,1)S(1)}, bf16[1,256,256]{2,1,0:T(8,128)(2,1)S(1)}, u32[]{:S(2)}, u32[]{:S(2)}) collective-permute-start(bf16[1,256,256]{2,1,0:T(8,128)(2,1)S(1)} %get-tuple-element.19), channel_id=1, source_target_pairs={{0,8},{2,10},{4,12},{6,14},{8,0},{10,2},{12,4},{14,6},{16,24},{18,... | collective-permute-start | bytes 393224 | tf_op jit(solution)/shard_map/ppermute | solution.py:13
  14.1 9.1 %collective-permute-start.9 = (bf16[1,256,256]{2,1,0:T(8,128)(2,1)S(1)}, bf16[1,256,256]{2,1,0:T(8,128)(2,1)S(1)}, u32[]{:S(2)}, u32[]{:S(2)}) collective-permute-start(bf16[1,256,256]{2,1,0:T(8,128)(2,1)S(1)} %get-tuple-element.18), channel_id=1, source_target_pairs={{0,4},{2,6},{4,0},{6,2},{8,12},{10,14},{12,8},{14,10},{16,20},{18,... | collective-permute-start | bytes 393224 | tf_op jit(solution)/shard_map/ppermute | solution.py:13
  14.4 11.5 %collective-permute-start.3 = (bf16[256,256]{1,0:T(8,128)(2,1)S(1)}, bf16[256,256]{1,0:T(8,128)(2,1)S(1)}, u32[]{:S(2)}, u32[]{:S(2)}) collective-permute-start(bf16[256,256]{1,0:T(8,128)(2,1)S(1)} %get-tuple-element.17), channel_id=1, source_target_pairs={{0,4},{2,6},{4,0},{6,2},{8,12},{10,14},{12,8},{14,10},{16,20},{18,... | collective-permute-start | bytes 393224 | tf_op jit(solution)/shard_map/ppermute | solution.py:13
  16.1 9.8 %collective-permute-start.4 = (bf16[256,256]{1,0:T(8,128)(2,1)S(1)}, bf16[256,256]{1,0:T(8,128)(2,1)S(1)}, u32[]{:S(2)}, u32[]{:S(2)}) collective-permute-start(bf16[256,256]{1,0:T(8,128)(2,1)S(1)} %get-tuple-element.21), channel_id=1, source_target_pairs={{0,12},{2,14},{4,8},{6,10},{8,4},{10,6},{12,0},{14,2},{16,28},{18,... | collective-permute-start | bytes 393224 | tf_op jit(solution)/shard_map/ppermute | solution.py:13
  17.8 9.3 %collective-permute-start.5 = (bf16[256,256]{1,0:T(8,128)(2,1)S(1)}, bf16[256,256]{1,0:T(8,128)(2,1)S(1)}, u32[]{:S(2)}, u32[]{:S(2)}) collective-permute-start(bf16[256,256]{1,0:T(8,128)(2,1)S(1)} %get-tuple-element.20), channel_id=1, source_target_pairs={{0,8},{2,10},{4,12},{6,14},{8,0},{10,2},{12,4},{14,6},{16,24},{18,... | collective-permute-start | bytes 393224 | tf_op jit(solution)/shard_map/ppermute | solution.py:13
  23.3 8.3 %collective-permute-start.10 = (bf16[256,256]{1,0:T(8,128)(2,1)S(1)}, bf16[256,256]{1,0:T(8,128)(2,1)S(1)}, u32[]{:S(2)}, u32[]{:S(2)}) collective-permute-start(bf16[256,256]{1,0:T(8,128)(2,1)S(1)} %fusion.16), channel_id=1, source_target_pairs={{0,16},{2,18},{4,20},{6,22},{8,24},{10,26},{12,28},{14,30},{16,0},... | collective-permute-start | bytes 393224 | tf_op jit(solution)/shard_map/ppermute | solution.py:13
